TPU v7x, 32 devices: a whole 2x2x4 slice. The times are simulated.
32 devices in a mesh: seq: 8 (over y, x, core), head: 4 (over z).
Axes of the slice: x: 2, y: 2, z: 4, core: 2. Of those that a mesh axis runs over, the one named last changes fastest.
Arguments:
- queries: bfloat16 [8192, 8192], P(('seq', 'head')), may hold values from -64 to 64
- key_rows: bfloat16 [8192, 1024], P(('seq', 'head')), may hold values from -6 to 6
- value_projection_rows: bfloat16 [8192, 1024], P(('seq', 'head')), may hold values from -6 to 6
- upstream: bfloat16 [8192, 8192], P(('seq', 'head')), may hold values from -6 to 6
- ancestors: int32 [128, 2], P('seq'), may hold values from -1 to 126, as said below
Outputs:
- attended: bfloat16 [8192, 8192], P(('seq', 'head'))
- query_grad: bfloat16 [8192, 8192], P(('seq', 'head'))
- key_grad: bfloat16 [8192, 1024], P(('seq', 'head'))
- value_grad: bfloat16 [8192, 1024], P(('seq', 'head'))
Inputs may be any that keep to these rules, and one draw needn't show every extreme that they name: `ancestors`: each entry of row b is -1 (no ancestor) or a block index from max(1, b - 32) to b - 1; where that range is not empty the first entry is b - 1, and where b is a multiple of 16 the last entry is the lowest index of that range. Entries of a row may repeat.
All inputs are finite; a program needn't handle non-finite values.
Results may differ from a plain program's by a relative error of at most 0.012.
The roundings to bfloat16 on the way count: a program that leaves them out, or rounds other values in their place, can miss the bound.
Values may be sent and summed in bfloat16 or wider, within the bound.
A program may use at most 192 MiB of HBM per device.

v0:
```python
import jax
import jax.numpy as jnp
from jax import lax
from jax.sharding import PartitionSpec as P

HEAD_SIZE = 128
MASK_BLOCK_SIZE = 64
ROOT = 64
ANC = 2


NEGATIVE = -1e30


def passed_along(x, axis, by):
    length = lax.axis_size(axis)
    pairs = [(i, i + by) for i in range(length) if 0 <= i + by < length]
    return lax.ppermute(x, axis, pairs)


def from_root(x, axis, root):
    mine = lax.axis_index(axis) == root
    return lax.psum(jnp.where(mine, x, jnp.zeros_like(x)), axis)


def block_scores(query_blocks, key_heads, shared):
    if shared:
        return jnp.einsum(
            "bqkgd,skd->bkgqs", query_blocks, key_heads, preferred_element_type=jnp.float32
        )
    return jnp.einsum(
        "bqkgd,bskd->bkgqs", query_blocks, key_heads, preferred_element_type=jnp.float32
    )


def block_apply(weights, rows_heads, shared):
    if shared:
        return jnp.einsum(
            "bkgqs,skd->bqkgd", weights, rows_heads, preferred_element_type=jnp.float32
        )
    return jnp.einsum("bkgqs,bskd->bqkgd", weights, rows_heads, preferred_element_type=jnp.float32)


def block_back(weights, query_side, shared):
    if shared:
        return jnp.einsum(
            "bkgqs,bqkgd->skd", weights, query_side, preferred_element_type=jnp.float32
        )
    return jnp.einsum("bkgqs,bqkgd->bskd", weights, query_side, preferred_element_type=jnp.float32)


def local(queries, key_rows, value_projection_rows, upstream, ancestors):
    local_query, local_key, local_value = (
        lax.all_to_all(queries, "head", split_axis=1, concat_axis=0, tiled=True),
        lax.all_to_all(key_rows, "head", split_axis=1, concat_axis=0, tiled=True),
        lax.all_to_all(value_projection_rows, "head", split_axis=1, concat_axis=0, tiled=True),
    )
    tokens = local_query.shape[0]
    nblocks = tokens // MASK_BLOCK_SIZE
    kv_width = local_key.shape[1]
    kv_heads = kv_width // HEAD_SIZE
    query_groups = local_query.shape[1] // HEAD_SIZE // kv_heads
    scale = HEAD_SIZE ** (-0.5)
    shard = lax.axis_index("seq")
    near_key, near_value = passed_along((local_key, local_value), "seq", 1)
    far_key, far_value = passed_along((local_key, local_value), "seq", 2)
    tree_root_key, tree_root_value = (
        from_root(local_key[:ROOT], "seq", 0),
        from_root(local_value[:ROOT], "seq", 0),
    )
    window_key = jnp.concatenate([far_key, near_key, local_key], 0).reshape(
        3 * nblocks, MASK_BLOCK_SIZE, kv_width
    )
    window_value = jnp.concatenate([far_value, near_value, local_value], 0).reshape(
        3 * nblocks, MASK_BLOCK_SIZE, kv_width
    )
    order = jnp.arange(ANC, dtype=jnp.int32)
    before = order[None, :] < order[:, None]
    repeated = jnp.any((ancestors[:, :, None] == ancestors[:, None, :]) & before[None], axis=2)
    valid = (ancestors >= 0) & jnp.logical_not(repeated)
    relative = jnp.clip(ancestors - (shard - 2) * nblocks, 0, 3 * nblocks - 1).reshape(-1)
    ancestor_key = jnp.take(window_key, relative, axis=0).reshape(
        nblocks, ANC * MASK_BLOCK_SIZE, kv_heads, HEAD_SIZE
    )
    ancestor_value = jnp.take(window_value, relative, axis=0).reshape(
        nblocks, ANC * MASK_BLOCK_SIZE, kv_heads, HEAD_SIZE
    )
    query_pos = (shard * tokens + jnp.arange(tokens, dtype=jnp.int32)).reshape(
        nblocks, MASK_BLOCK_SIZE
    )
    root_pos = jnp.arange(ROOT, dtype=jnp.int32)
    root_mask = root_pos[None, None, :] <= query_pos[:, :, None]
    own_mask = (query_pos[:, None, :] <= query_pos[:, :, None]) & (query_pos[:, None, :] >= ROOT)
    anc_mask = jnp.broadcast_to(
        jnp.repeat(valid, MASK_BLOCK_SIZE, axis=1)[:, None, :],
        (nblocks, MASK_BLOCK_SIZE, ANC * MASK_BLOCK_SIZE),
    )
    sections = [
        (
            tree_root_key.reshape(ROOT, kv_heads, HEAD_SIZE),
            tree_root_value.reshape(ROOT, kv_heads, HEAD_SIZE),
            root_mask,
            True,
        ),
        (
            local_key.reshape(nblocks, MASK_BLOCK_SIZE, kv_heads, HEAD_SIZE),
            local_value.reshape(nblocks, MASK_BLOCK_SIZE, kv_heads, HEAD_SIZE),
            own_mask,
            False,
        ),
        (ancestor_key, ancestor_value, anc_mask, False),
    ]
    query_blocks = local_query.reshape(nblocks, MASK_BLOCK_SIZE, kv_heads, query_groups, HEAD_SIZE)
    masked_list = []
    row_max = jnp.full((nblocks, kv_heads, query_groups, MASK_BLOCK_SIZE), NEGATIVE, jnp.float32)
    row_sum = jnp.zeros((nblocks, kv_heads, query_groups, MASK_BLOCK_SIZE), jnp.float32)
    for entry in sections:
        wide_mask = entry[2][:, None, None]
        masked = jnp.where(
            wide_mask, block_scores(query_blocks, entry[0], entry[3]) * scale, NEGATIVE
        )
        sect_max = jnp.max(masked, axis=-1)
        sect_sum = jnp.sum(
            jnp.where(wide_mask, jnp.exp(masked - sect_max[..., None]), 0.0), axis=-1
        )
        new_max = jnp.maximum(row_max, sect_max)
        row_sum = row_sum * jnp.exp(row_max - new_max) + sect_sum * jnp.exp(sect_max - new_max)
        row_max = new_max
        masked_list.append(masked)
    lse = (row_max + jnp.log(row_sum))[..., None]
    prob_list = []
    out_sum = jnp.zeros((nblocks, MASK_BLOCK_SIZE, kv_heads, query_groups, HEAD_SIZE), jnp.float32)
    for number in range(3):
        entry = sections[number]
        probs = jnp.where(entry[2][:, None, None], jnp.exp(masked_list[number] - lse), 0.0).astype(
            jnp.bfloat16
        )
        prob_list.append(probs)
        out_sum = out_sum + block_apply(probs, entry[1], entry[3])
    attended_heads = lax.optimization_barrier(out_sum.astype(jnp.bfloat16))
    attended = lax.all_to_all(
        attended_heads.reshape(tokens, -1), "head", split_axis=0, concat_axis=1, tiled=True
    )
    local_upstream = lax.all_to_all(upstream, "head", split_axis=1, concat_axis=0, tiled=True)
    upstream_blocks = local_upstream.reshape(
        nblocks, MASK_BLOCK_SIZE, kv_heads, query_groups, HEAD_SIZE
    )
    delta = jnp.sum(
        upstream_blocks.astype(jnp.float32) * attended_heads.astype(jnp.float32), axis=-1
    ).transpose(0, 2, 3, 1)[..., None]
    query_sum = jnp.zeros(
        (nblocks, MASK_BLOCK_SIZE, kv_heads, query_groups, HEAD_SIZE), jnp.float32
    )
    key_parts = []
    value_parts = []
    for number in range(3):
        entry = sections[number]
        probs = prob_list[number]
        dprob = block_scores(upstream_blocks, entry[1], entry[3])
        dscore = (probs.astype(jnp.float32) * (dprob - delta)).astype(jnp.bfloat16)
        query_sum = query_sum + block_apply(dscore, entry[0], entry[3])
        key_parts.append(scale * block_back(dscore, query_blocks, entry[3]))
        value_parts.append(block_back(probs, upstream_blocks, entry[3]))
    root_key_grad, root_value_grad = lax.psum(
        (key_parts[0].reshape(ROOT, kv_width), value_parts[0].reshape(ROOT, kv_width)), "seq"
    )
    own_key = key_parts[1].reshape(tokens, kv_width)
    own_value = value_parts[1].reshape(tokens, kv_width)
    anc_both = jnp.concatenate(
        [
            key_parts[2].reshape(nblocks * ANC, MASK_BLOCK_SIZE * kv_width),
            value_parts[2].reshape(nblocks * ANC, MASK_BLOCK_SIZE * kv_width),
        ],
        1,
    )
    placing = (jnp.arange(3 * nblocks, dtype=jnp.int32)[:, None] == relative[None, :]).astype(
        jnp.float32
    )
    window_both = jnp.dot(
        placing, anc_both, precision=lax.Precision.HIGHEST, preferred_element_type=jnp.float32
    )
    window_grad_key = window_both[:, : MASK_BLOCK_SIZE * kv_width].reshape(3 * tokens, kv_width)
    window_grad_value = window_both[:, MASK_BLOCK_SIZE * kv_width :].reshape(3 * tokens, kv_width)
    far_key_grad, far_value_grad = (window_grad_key[:tokens], window_grad_value[:tokens])
    near_key_grad, near_value_grad = (
        window_grad_key[tokens : 2 * tokens],
        window_grad_value[tokens : 2 * tokens],
    )
    self_key_grad, self_value_grad = (
        window_grad_key[2 * tokens :],
        window_grad_value[2 * tokens :],
    )
    one_key, one_value = passed_along((near_key_grad, near_value_grad), "seq", -1)
    two_key, two_value = (
        passed_along(far_key_grad.astype(jnp.bfloat16), "seq", -2).astype(far_key_grad.dtype),
        passed_along(far_value_grad.astype(jnp.bfloat16), "seq", -2).astype(far_value_grad.dtype),
    )
    back_key = one_key + two_key
    back_value = one_value + two_value
    first_shard = shard == 0
    root_key_full = jnp.zeros((tokens, kv_width), jnp.float32).at[:ROOT].set(root_key_grad)
    root_value_full = jnp.zeros((tokens, kv_width), jnp.float32).at[:ROOT].set(root_value_grad)
    key_total = own_key + self_key_grad + back_key + jnp.where(first_shard, root_key_full, 0.0)
    value_total = (
        own_value + self_value_grad + back_value + jnp.where(first_shard, root_value_full, 0.0)
    )
    query_local = (scale * query_sum).astype(jnp.bfloat16).reshape(tokens, -1)
    query_grad, key_grad, value_grad = (
        lax.all_to_all(query_local, "head", split_axis=0, concat_axis=1, tiled=True),
        lax.all_to_all(
            key_total.astype(jnp.bfloat16), "head", split_axis=0, concat_axis=1, tiled=True
        ),
        lax.all_to_all(
            value_total.astype(jnp.bfloat16), "head", split_axis=0, concat_axis=1, tiled=True
        ),
    )
    return (attended, query_grad, key_grad, value_grad)


def solution(mesh):
    placed = (
        P(("seq", "head"), None),
        P(("seq", "head"), None),
        P(("seq", "head"), None),
        P(("seq", "head"), None),
        P("seq", None),
    )
    return jax.shard_map(
        local,
        mesh=mesh,
        in_specs=placed,
        out_specs=(
            P(("seq", "head"), None),
            P(("seq", "head"), None),
            P(("seq", "head"), None),
            P(("seq", "head"), None),
        ),
        check_vma=False,
    )
```

profile of v0, /device:TPU:0, one launch (start us, length us, event | category | flops | bytes accessed | tf_op | source)
XLA Modules:
  0.0 652.4 jit_solution(6052750993636207971)
XLA Ops:
  9.0 6.3 all-to-all-start.1
  17.2 12.6 %all-to-all-done.1 = bf16[256,4,256]{2,0,1:T(8,128)(2,1)S(1)} async-done(((bf16[256,4,256]{2,0,1:T(8,128)(2,1)}), bf16[256,4,256]{2,0,1:T(8,128)(2,1)S(1)}, u32[]{:S(2)}, u32[]{:S(2)}) %all-to-all-start.1) | async-done | bytes 524320 | tf_op jit(solution)/shard_map/all_to_all | solution.py:55
  38.1 9.2 %all-to-all-done = bf16[256,4,256]{2,0,1:T(8,128)(2,1)S(1)} async-done(((bf16[256,4,256]{2,0,1:T(8,128)(2,1)}), bf16[256,4,256]{2,0,1:T(8,128)(2,1)S(1)}, u32[]{:S(2)}, u32[]{:S(2)}) %all-to-all-start) | async-done | bytes 524320 | tf_op jit(solution)/shard_map/all_to_all | solution.py:56
  78.4 7.6 %collective-permute-done.2 = bf16[1024,256]{1,0:T(8,128)(2,1)} collective-permute-done((bf16[1024,256]{1,0:T(8,128)(2,1)S(1)}, bf16[1024,256]{1,0:T(8,128)(2,1)}, u32[]{:S(2)}, u32[]{:S(2)}) %collective-permute-start.2) | collective-permute-done | bytes 524320 | tf_op jit(solution)/shard_map/ppermute | solution.py:18
  92.9 52.1 %all-to-all-done.2 = bf16[256,4,2048]{2,0,1:T(8,128)(2,1)} async-done(((bf16[256,4,2048]{2,0,1:T(8,128)(2,1)}), bf16[256,4,2048]{2,0,1:T(8,128)(2,1)}, u32[]{:S(2)}, u32[]{:S(2)}) %all-to-all-start.2) | async-done | bytes 4194336 | tf_op jit(solution)/shard_map/all_to_all | solution.py:54
  149.9 5.7 copy.384
  155.6 8.5 %bitcast_reduce_fusion = (f32[16,2,8,64]{3,2,1,0:T(8,128)}, f32[16,2,128,64,8]{2,3,4,1,0:T(8,128)}) fusion(pred[16,128]{1,0:T(8,128)(4,1)S(1)} %broadcast_in_dim_reshape.2, bf16[16,64,2,8,128]{4,3,2,1,0:T(8,128)(2,1)} %bitcast.91, bf16[16,128,2,128,1]{3,2,1,0,4:T(2,128)(2,1)S(1)} %bitcast.263), kind=kOutput, calls=%fused_computation.20 | convolution fusion | flops 543145984 | bytes 13699072 | tf_op jit(solution)/shard_map/bqkgd,bskd->bkgqs/dot_general | solution.py:31
  164.1 6.1 fusion.15
  173.1 6.1 fusion.16
  191.4 5.5 fusion.127
  196.8 5.2 fusion.14
  206.7 9.6 %fusion.8 = bf16[16,64,2,8,128]{4,1,3,0,2:T(8,128)(2,1)} fusion(f32[16,2,128,8,64]{2,4,3,0,1:T(8,128)} %fusion.31, f32[2,128,16,8,64]{1,4,3,2,0:T(8,128)} %fusion.127, bf16[16,2,8,64,64]{3,4,2,0,1:T(8,128)(2,1)S(1)} %get-tuple-element.55, bf16[16,64,2,128,1]{3,2,1,0,4:T(2,128)(2,1)S(1)} %bitcast.255), kind=kOutput, calls=%fused_computation.16 | convolution fusion | flops 274726912 | bytes 23592960 | tf_op jit(solution)/shard_map/bkgqs,bskd->bqkgd/dot_general | solution.py:41
  216.3 26.2 %all-to-all-done.4 = bf16[256,4,2048]{2,0,1:T(8,128)(2,1)} async-done(((bf16[256,4,2048]{2,0,1:T(8,128)(2,1)}), bf16[256,4,2048]{2,0,1:T(8,128)(2,1)}, u32[]{:S(2)}, u32[]{:S(2)}) %all-to-all-start.4) | async-done | bytes 4194336 | tf_op jit(solution)/shard_map/all_to_all | solution.py:144
  253.2 6.7 %fusion.3 = bf16[16,2,8,64,128]{4,3,2,1,0:T(8,128)(2,1)} fusion(bf16[16,2,8,64,128]{4,3,2,1,0:T(8,128)(2,1)} %copy-done.6, bf16[16,64,2,8,128]{4,3,2,1,0:T(8,128)(2,1)S(1)} %bitcast.230, bf16[16,128,2,128,1]{3,2,1,0,4:T(2,128)(2,1)S(1)} %bitcast.242, f32[16,64,2,8]{1,3,0,2:T(8,128)S(1)} %multiply_reduce_fusion), kind=kOutput, calls=%fused_computation.7 | convolution fusion | flops 545259520 | bytes 13697024 | tf_op jit(solution)/shard_map/bqkgd,bskd->bkgqs/dot_general | solution.py:31
  259.9 7.9 %fusion.5 = bf16[16,2,8,64,64]{3,4,2,0,1:T(8,128)(2,1)} fusion(bf16[16,2,8,64,64]{3,4,2,0,1:T(8,128)(2,1)} %copy-done.3, f32[16,2,8,64]{3,2,0,1:T(8,128)S(1)} %bitcast.265, bf16[16,64,2,8,128]{4,3,2,1,0:T(8,128)(2,1)S(1)} %bitcast.231, bf16[16,64,2,128,1]{3,2,1,0,4:T(2,128)(2,1)S(1)} %bitcast.256), kind=kOutput, calls=%fused_computation.11 | convolution fusion | flops 272629760 | bytes 8978432 | tf_op jit(solution)/shard_map/bqkgd,bskd->bkgqs/dot_general | solution.py:31
  267.8 5.6 fusion.7
  306.0 6.1 fusion.71
  337.1 13.6 %collective-permute-done.7 = bf16[1024,256]{1,0:T(8,128)(2,1)} collective-permute-done((bf16[1024,256]{1,0:T(8,128)(2,1)}, bf16[1024,256]{1,0:T(8,128)(2,1)}, u32[]{:S(2)}, u32[]{:S(2)}) %collective-permute-start.7) | collective-permute-done | bytes 524320 | tf_op jit(solution)/shard_map/ppermute | solution.py:18
  352.3 40.7 %all-reduce.5.cloned.1.call-done = (f32[64,256]{1,0:T(8,128)}, f32[64,256]{1,0:T(8,128)}) async-done(((f32[64,256]{1,0:T(8,128)}, f32[64,256]{1,0:T(8,128)}), (f32[64,256]{1,0:T(8,128)}, f32[64,256]{1,0:T(8,128)})) %all-reduce.5.cloned.1.call-update) | async-done | bytes 131088 | tf_op jit(solution)/shard_map/psum | solution.py:164
  399.4 7.4 %fusion.129 = f32[2,128,16,8,64]{1,4,3,2,0:T(8,128)} fusion(bf16[16,2,8,64,64]{3,4,2,0,1:T(8,128)(2,1)} %fusion.7, bf16[64,2,128]{2,0,1:T(8,128)(2,1)S(1)} %copy-done.28), kind=kOutput, calls=%fused_computation.140 | convolution fusion | flops 268435456 | bytes 10518528 | tf_op jit(solution)/shard_map/bkgqs,skd->bqkgd/dot_general | solution.py:38
  412.3 5.2 all-to-all-start.7
  417.4 9.0 %fusion.1 = bf16[16,64,2,8,128]{4,1,3,0,2:T(8,128)(2,1)S(1)} fusion(f32[16,2,128,8,64]{2,4,3,0,1:T(8,128)} %fusion.29, f32[2,128,16,8,64]{1,4,3,2,0:T(8,128)} %fusion.129, bf16[16,2,8,64,64]{3,4,2,0,1:T(8,128)(2,1)} %fusion.5, bf16[16,64,2,128,1]{3,2,1,0,4:T(2,128)(2,1)S(1)} %bitcast.254), kind=kOutput, calls=%fused_computation.4 | convolution fusion | flops 276824064 | bytes 23592960 | tf_op jit(solution)/shard_map/bkgqs,bskd->bqkgd/dot_general | solution.py:41
  426.5 5.6 copy.313
  432.1 7.3 %all_to_all.126 = bf16[4,256,2048]{2,1,0:T(8,128)(2,1)} reshape(bf16[16,64,2,8,128]{4,3,2,1,0:T(8,128)(2,1)} %copy.313) | data formatting | bytes 8388608 | tf_op jit(solution)/shard_map/all_to_all | solution.py:209
  444.5 7.7 %copy.298 = bf16[16,64,2,8,128]{4,3,2,1,0:T(8,128)(2,1)} copy(bf16[16,64,2,8,128]{4,1,3,0,2:T(8,128)(2,1)} %fusion.8) | data formatting | bytes 8388608 | tf_op jit(solution)/shard_map/optimization_barrier | solution.py:140
  452.2 7.3 %all_to_all.119 = bf16[4,256,2048]{2,1,0:T(8,128)(2,1)} reshape(bf16[16,64,2,8,128]{4,3,2,1,0:T(8,128)(2,1)} %copy.298) | data formatting | bytes 8388608 | tf_op jit(solution)/shard_map/all_to_all | solution.py:141
  459.5 75.8 %all-to-all-done.5 = bf16[4,256,2048]{2,1,0:T(8,128)(2,1)} async-done(((bf16[4,256,2048]{2,1,0:T(8,128)(2,1)}), bf16[4,256,2048]{2,1,0:T(8,128)(2,1)}, u32[]{:S(2)}, u32[]{:S(2)}) %all-to-all-start.5) | async-done | bytes 4194336 | tf_op jit(solution)/shard_map/all_to_all | solution.py:209
  541.9 6.2 copy.314
  548.1 6.3 copy.334
  554.4 78.4 %all-to-all-done.3 = bf16[4,256,2048]{2,1,0:T(8,128)(2,1)} async-done(((bf16[4,256,2048]{2,1,0:T(8,128)(2,1)}), bf16[4,256,2048]{2,1,0:T(8,128)(2,1)}, u32[]{:S(2)}, u32[]{:S(2)}) %all-to-all-start.3) | async-done | bytes 4194336 | tf_op jit(solution)/shard_map/all_to_all | solution.py:141
  632.8 6.2 copy.299
  639.0 6.3 copy.333
  (162 shorter events, 167.5 us)
Async XLA Ops:
  9.0 20.8 %all-to-all-start.1 = ((bf16[256,4,256]{2,0,1:T(8,128)(2,1)}), bf16[256,4,256]{2,0,1:T(8,128)(2,1)S(1)}, u32[]{:S(2)}, u32[]{:S(2)}) async-start(bf16[256,4,256]{2,0,1:T(8,128)(2,1)} %bitcast.224), calls=%async_computation.1 | async-start | bytes 1048576 | tf_op jit(solution)/shard_map/all_to_all | solution.py:55
  29.8 17.4 %all-to-all-start = ((bf16[256,4,256]{2,0,1:T(8,128)(2,1)}), bf16[256,4,256]{2,0,1:T(8,128)(2,1)S(1)}, u32[]{:S(2)}, u32[]{:S(2)}) async-start(bf16[256,4,256]{2,0,1:T(8,128)(2,1)} %bitcast.225), calls=%async_computation | async-start | bytes 1048576 | tf_op jit(solution)/shard_map/all_to_all | solution.py:56
  47.3 97.7 %all-to-all-start.2 = ((bf16[256,4,2048]{2,0,1:T(8,128)(2,1)}), bf16[256,4,2048]{2,0,1:T(8,128)(2,1)}, u32[]{:S(2)}, u32[]{:S(2)}) async-start(bf16[256,4,2048]{2,0,1:T(8,128)(2,1)} %bitcast.238), calls=%async_computation.2 | async-start | bytes 8388608 | tf_op jit(solution)/shard_map/all_to_all | solution.py:54
  52.3 111.8 %all-reduce.7.cloned.1.call-start = ((), (), s32[]{:S(2)}) async-start(), calls=%async_computation.9 | async-start | bytes 131072 | tf_op jit(solution)/shard_map/psum | solution.py:23
  58.7 111.5 %copy-start.23 = (pred[16,64,64]{1,2,0:T(8,128)(4,1)}, pred[16,64,64]{1,2,0:T(8,128)(4,1)S(1)}, u32[]{:S(2)}) copy-start(pred[16,64,64]{1,2,0:T(8,128)(4,1)S(1)} %get-tuple-element.58) | copy-start | bytes 196612
  58.7 15.9 %collective-permute-start = (bf16[1024,256]{1,0:T(8,128)(2,1)S(1)}, bf16[1024,256]{1,0:T(8,128)(2,1)S(1)}, u32[]{:S(2)}, u32[]{:S(2)}) collective-permute-start(bf16[1024,256]{1,0:T(8,128)(2,1)S(1)} %bitcast.248), channel_id=1, source_target_pairs={{0,8},{4,12},{8,16},{12,20},{16,24},{20,28},{1,9},{5,13},{9,17},{1... | collective-permute-start | bytes 1572872 | tf_op jit(solution)/shard_map/ppermute | solution.py:18
  62.2 13.3 %collective-permute-start.1 = (bf16[1024,256]{1,0:T(8,128)(2,1)S(1)}, bf16[1024,256]{1,0:T(8,128)(2,1)}, u32[]{:S(2)}, u32[]{:S(2)}) collective-permute-start(bf16[1024,256]{1,0:T(8,128)(2,1)S(1)} %bitcast.249), channel_id=1, source_target_pairs={{0,4},{4,8},{8,12},{12,16},{16,20},{20,24},{24,28},{1,5},{5,9},{9,... | collective-permute-start | bytes 1572872 | tf_op jit(solution)/shard_map/ppermute | solution.py:18
  64.3 21.7 %collective-permute-start.2 = (bf16[1024,256]{1,0:T(8,128)(2,1)S(1)}, bf16[1024,256]{1,0:T(8,128)(2,1)}, u32[]{:S(2)}, u32[]{:S(2)}) collective-permute-start(bf16[1024,256]{1,0:T(8,128)(2,1)S(1)} %bitcast.243), channel_id=1, source_target_pairs={{0,8},{4,12},{8,16},{12,20},{16,24},{20,28},{1,9},{5,13},{9,17},{1... | collective-permute-start | bytes 1572872 | tf_op jit(solution)/shard_map/ppermute | solution.py:18
  68.3 17.7 %collective-permute-start.3 = (bf16[1024,256]{1,0:T(8,128)(2,1)S(1)}, bf16[1024,256]{1,0:T(8,128)(2,1)}, u32[]{:S(2)}, u32[]{:S(2)}) collective-permute-start(bf16[1024,256]{1,0:T(8,128)(2,1)S(1)} %bitcast.244), channel_id=1, source_target_pairs={{0,4},{4,8},{8,12},{12,16},{16,20},{20,24},{24,28},{1,5},{5,9},{9,... | collective-permute-start | bytes 1572872 | tf_op jit(solution)/shard_map/ppermute | solution.py:18
  72.4 100.7 %copy-start.12 = (bf16[16,64,2,128]{3,2,1,0:T(2,128)(2,1)}, bf16[16,64,2,128]{3,2,1,0:T(2,128)(2,1)S(1)}, u32[]{:S(2)}) copy-start(bf16[16,64,2,128]{3,2,1,0:T(2,128)(2,1)S(1)} %reshape.247) | copy-start | bytes 1572868
  145.0 97.5 %all-to-all-start.4 = ((bf16[256,4,2048]{2,0,1:T(8,128)(2,1)}), bf16[256,4,2048]{2,0,1:T(8,128)(2,1)}, u32[]{:S(2)}, u32[]{:S(2)}) async-start(bf16[256,4,2048]{2,0,1:T(8,128)(2,1)} %bitcast.237), calls=%async_computation.4 | async-start | bytes 8388608 | tf_op jit(solution)/shard_map/all_to_all | solution.py:144
  149.8 243.2 %all-reduce.5.cloned.1.call-start = ((), (), s32[]{:S(2)}) async-start(), calls=%async_computation.8 | async-start | bytes 262144 | tf_op jit(solution)/shard_map/psum | solution.py:164
  170.2 11.9 %slice-start = ((s8[8388608]{0:T(1024)(128)(4,1)}), s8[4194304]{0:T(1024)(128)(4,1)S(1)}, s32[]{:S(2)}) async-start(s8[8388608]{0:T(1024)(128)(4,1)} %bitcast.235), calls=%async_computation.10 | async-start | bytes 8388608
  173.1 9.0 %slice-start.1 = ((s8[8388608]{0:T(1024)(128)(4,1)}), s8[4194304]{0:T(1024)(128)(4,1)S(1)}, s32[]{:S(2)}) async-start(s8[8388608]{0:T(1024)(128)(4,1)} %bitcast.235), calls=%async_computation.11 | async-start | bytes 8388608
  191.4 15.3 %copy-start.3 = (bf16[16,2,8,64,64]{3,4,2,0,1:T(8,128)(2,1)}, bf16[16,2,8,64,64]{3,4,2,0,1:T(8,128)(2,1)S(1)}, u32[]{:S(2)}) copy-start(bf16[16,2,8,64,64]{3,4,2,0,1:T(8,128)(2,1)S(1)} %get-tuple-element.55) | copy-start | bytes 6291460
  246.3 27.1 %copy-start = (bf16[128,8,16,128]{3,2,1,0:T(8,128)(2,1)}, bf16[128,8,16,128]{3,2,1,0:T(8,128)(2,1)S(1)}, u32[]{:S(2)}) copy-start(bf16[128,8,16,128]{3,2,1,0:T(8,128)(2,1)S(1)} %copy.385) | copy-start | bytes 12582916
  259.9 7.9 %copy-start.2 = (bf16[16,2,8,64,64]{3,4,2,0,1:T(8,128)(2,1)S(1)}, bf16[16,2,8,64,64]{3,4,2,0,1:T(8,128)(2,1)}, u32[]{:S(2)}) copy-start(bf16[16,2,8,64,64]{3,4,2,0,1:T(8,128)(2,1)} %copy-done.1) | copy-start | bytes 6291460
  300.2 34.9 %collective-permute-start.4 = (f32[1024,256]{1,0:T(8,128)}, f32[1024,256]{1,0:T(8,128)}, u32[]{:S(2)}, u32[]{:S(2)}) collective-permute-start(f32[1024,256]{1,0:T(8,128)} %slice.87), channel_id=1, source_target_pairs={{4,0},{8,4},{12,8},{16,12},{20,16},{24,20},{28,24},{5,1},{9,5},{13... | collective-permute-start | bytes 3145736 | tf_op jit(solution)/shard_map/ppermute | solution.py:18
  304.6 7.5 %copy-start.20 = (f32[16,16384]{1,0:T(8,128)S(1)}, f32[16,16384]{1,0:T(8,128)}, u32[]{:S(2)}) copy-start(f32[16,16384]{1,0:T(8,128)} %get-tuple-element.49) | copy-start | bytes 3145732
  304.6 30.4 %collective-permute-start.5 = (bf16[1024,256]{1,0:T(8,128)(2,1)}, bf16[1024,256]{1,0:T(8,128)(2,1)}, u32[]{:S(2)}, u32[]{:S(2)}) collective-permute-start(bf16[1024,256]{1,0:T(8,128)(2,1)} %convert_element_type.73), channel_id=1, source_target_pairs={{8,0},{12,4},{16,8},{20,12},{24,16},{28,20},{9,1},{13,5},{17,9},{2... | collective-permute-start | bytes 1572872 | tf_op jit(solution)/shard_map/ppermute | solution.py:18
  313.3 37.4 %collective-permute-start.6 = (f32[1024,256]{1,0:T(8,128)}, f32[1024,256]{1,0:T(8,128)}, u32[]{:S(2)}, u32[]{:S(2)}) collective-permute-start(f32[1024,256]{1,0:T(8,128)} %slice.92), channel_id=1, source_target_pairs={{4,0},{8,4},{12,8},{16,12},{20,16},{24,20},{28,24},{5,1},{9,5},{13... | collective-permute-start | bytes 3145736 | tf_op jit(solution)/shard_map/ppermute | solution.py:18
  320.8 6.5 copy-start.19
  320.8 29.9 %collective-permute-start.7 = (bf16[1024,256]{1,0:T(8,128)(2,1)}, bf16[1024,256]{1,0:T(8,128)(2,1)}, u32[]{:S(2)}, u32[]{:S(2)}) collective-permute-start(bf16[1024,256]{1,0:T(8,128)(2,1)} %convert_element_type.76), channel_id=1, source_target_pairs={{8,0},{12,4},{16,8},{20,12},{24,16},{28,20},{9,1},{13,5},{17,9},{2... | collective-permute-start | bytes 1572872 | tf_op jit(solution)/shard_map/ppermute | solution.py:18
  335.1 15.6 %copy-start.15 = (f32[16,64,2,128]{3,2,1,0:T(2,128)S(1)}, f32[16,64,2,128]{3,2,1,0:T(2,128)}, u32[]{:S(2)}) copy-start(f32[16,64,2,128]{3,2,1,0:T(2,128)} %copy.328) | copy-start | bytes 3145732
  337.1 62.3 %copy-start.28 = (bf16[64,2,128]{2,0,1:T(8,128)(2,1)S(1)}, bf16[64,2,128]{2,0,1:T(8,128)(2,1)}, u32[]{:S(2)}) copy-start(bf16[64,2,128]{2,0,1:T(8,128)(2,1)} %get-tuple-element.47) | copy-start | bytes 98308
  394.8 17.5 %all-to-all-start.6 = ((bf16[4,256,256]{2,1,0:T(8,128)(2,1)}), bf16[4,256,256]{2,1,0:T(8,128)(2,1)S(1)}, u32[]{:S(2)}, u32[]{:S(2)}) async-start(bf16[4,256,256]{2,1,0:T(8,128)(2,1)} %bitcast.53), calls=%async_computation.6 | async-start | bytes 1048576 | tf_op jit(solution)/shard_map/all_to_all | solution.py:210
  399.4 7.4 %copy-start.9 = (bf16[16,2,8,64,128]{4,3,2,1,0:T(8,128)(2,1)S(1)}, bf16[16,2,8,64,128]{4,3,2,1,0:T(8,128)(2,1)}, u32[]{:S(2)}) copy-start(bf16[16,2,8,64,128]{4,3,2,1,0:T(8,128)(2,1)} %fusion.3) | copy-start | bytes 12582916
  399.4 7.4 %copy-start.17 = (bf16[16,128,2,128]{3,2,1,0:T(2,128)(2,1)S(1)}, bf16[16,128,2,128]{3,2,1,0:T(2,128)(2,1)}, u32[]{:S(2)}) copy-start(bf16[16,128,2,128]{3,2,1,0:T(2,128)(2,1)} %reshape.250) | copy-start | bytes 3145732
  406.8 10.7 %copy-start.13 = (bf16[16,64,2,128]{3,2,1,0:T(2,128)(2,1)S(1)}, bf16[16,64,2,128]{3,2,1,0:T(2,128)(2,1)}, u32[]{:S(2)}) copy-start(bf16[16,64,2,128]{3,2,1,0:T(2,128)(2,1)} %copy-done.12) | copy-start | bytes 1572868
  412.3 27.1 %all-to-all-start.7 = ((bf16[4,256,256]{2,1,0:T(8,128)(2,1)}), bf16[4,256,256]{2,1,0:T(8,128)(2,1)S(1)}, u32[]{:S(2)}, u32[]{:S(2)}) async-start(bf16[4,256,256]{2,1,0:T(8,128)(2,1)} %bitcast.61), calls=%async_computation.7 | async-start | bytes 1048576 | tf_op jit(solution)/shard_map/all_to_all | solution.py:213
  439.4 95.9 %all-to-all-start.5 = ((bf16[4,256,2048]{2,1,0:T(8,128)(2,1)}), bf16[4,256,2048]{2,1,0:T(8,128)(2,1)}, u32[]{:S(2)}, u32[]{:S(2)}) async-start(bf16[4,256,2048]{2,1,0:T(8,128)(2,1)} %all_to_all.126), calls=%async_computation.5 | async-start | bytes 8388608 | tf_op jit(solution)/shard_map/all_to_all | solution.py:209
  535.3 97.5 %all-to-all-start.3 = ((bf16[4,256,2048]{2,1,0:T(8,128)(2,1)}), bf16[4,256,2048]{2,1,0:T(8,128)(2,1)}, u32[]{:S(2)}, u32[]{:S(2)}) async-start(bf16[4,256,2048]{2,1,0:T(8,128)(2,1)} %all_to_all.119), calls=%async_computation.3 | async-start | bytes 8388608 | tf_op jit(solution)/shard_map/all_to_all | solution.py:141
  (19 other events, 81.3 us)
Sparse Core Ops, SparseCore 0:
  74.8 52.4 all-reduce.6
  335.2 57.8 all-reduce.4
where the time goes:
time: 660 us; the launch traced here: 652 us
  waiting for transfers between devices  316 us (48%)
  local copies, waits for them, and re-layouts  114 us (17%)
  matrix products  113 us (17%)
  starting transfers between devices  58.5 us (9%)
  other arithmetic  35.4 us (5%)
  between operations  14.9 us (2%)
    all_to_all x1, waiting for transfers between devices, local(): lax.all_to_all(attended_heads.reshape(tokens, -1), 'head', split_axis=0,...  78.4 us
    all_to_all x1, waiting for transfers between devices, local(): lax.all_to_all(query_local, 'head', split_axis=0, concat_axis=1, tiled=True)  75.8 us
    all_to_all x1, waiting for transfers between devices, local(): lax.all_to_all(queries, 'head', split_axis=1, concat_axis=0, tiled=True)  52.1 us
    psum x1, waiting for transfers between devices, local(): lax.psum((key_parts[0].reshape(ROOT, kv_width), value_parts[0].reshape(RO...  40.7 us
    dot_general x4, matrix products, block_scores(): jnp.einsum('bqkgd,bskd->bkgqs', query_blocks, key_heads, preferred_elemen...  29.2 us
    dot_general x4, matrix products, block_apply(): jnp.einsum('bkgqs,bskd->bqkgd', weights, rows_heads, preferred_element_ty...  27.7 us
    all_to_all x1, waiting for transfers between devices, local(): lax.all_to_all(upstream, 'head', split_axis=1, concat_axis=0, tiled=True)  26.2 us
    unnamed x70, local copies, waits for them, and re-layouts  24.1 us
  transfers between devices with their start and end apart: 18, of which 10 were waited for; matrix products, arithmetic and copies ran while one was open for 27% of the time, Pallas kernels for 0%

commit v1 on v0

v1 whole, which is shorter than its diff:
```python
import functools
import math

import jax
import jax.numpy as jnp
from jax import lax
from jax.experimental import pallas as pl
from jax.experimental.pallas import tpu as pltpu
from jax.sharding import PartitionSpec as P

HEAD_SIZE = 128
BLOCK = 64
NEGATIVE = -1e30
CHUNKS = 2


def shifted(x, axis, by):
    length = lax.axis_size(axis)
    pairs = [(i, i + by) for i in range(length) if 0 <= i + by < length]
    return lax.ppermute(x, axis, pairs)


def spread_from_first(x, axis):
    length = lax.axis_size(axis)
    step = 1
    while step < length:
        pairs = [(i, i + step) for i in range(step) if i + step < length]
        x = x + lax.ppermute(x, axis, pairs)
        step *= 2
    return x


def sum_to_first(x, axis):
    length = lax.axis_size(axis)
    step = 1
    while step < length:
        step *= 2
    while step > 1:
        step //= 2
        pairs = [(i + step, i) for i in range(step) if i + step < length]
        x = x + lax.ppermute(x, axis, pairs)
    return x


def attention_kernel(
    info, q_ref, up_ref, own_ref, before_ref, edge_ref, root_ref, rand_ref, *rest, groups, aliased
):
    if aliased:
        rest = rest[2:]
    att_ref, dq_ref, g_own, g_prev, g_rand, g_root = rest
    j = pl.program_id(1)
    scale = HEAD_SIZE ** (-0.5)
    first = info[0] + j == 0
    rows = groups * BLOCK
    q = jnp.concatenate(
        [q_ref[:, r * HEAD_SIZE : (r + 1) * HEAD_SIZE] for r in range(groups)], axis=0
    )
    up = jnp.concatenate(
        [up_ref[:, r * HEAD_SIZE : (r + 1) * HEAD_SIZE] for r in range(groups)], axis=0
    )
    prev = jnp.where(j == 0, edge_ref[0], before_ref[0])
    keys = jnp.concatenate([root_ref[0, 0], own_ref[0, 0], prev[0], rand_ref[0, 0]], axis=0)
    values = jnp.concatenate([root_ref[0, 1], own_ref[0, 1], prev[1], rand_ref[0, 1]], axis=0)
    up_t = up.T
    scores = lax.dot_general(
        keys, q, (((1,), (1,)), ((), ())), preferred_element_type=jnp.float32
    ) * (scale * math.log2(math.e))
    key_at = lax.broadcasted_iota(jnp.int32, (BLOCK, rows), 0)
    query_at = lax.broadcasted_iota(jnp.int32, (BLOCK, rows), 1) & (BLOCK - 1)
    causal = key_at <= query_at
    never = jnp.float32(NEGATIVE)
    zero = jnp.float32(0.0)
    root_off = jnp.where(causal, zero, jnp.where(first, never, zero))
    own_off = jnp.where(causal, jnp.where(first, never, zero), never)
    prev_off = jnp.where(info[1 + 2 * j] > 0, zero, never)
    rand_off = jnp.where(info[2 + 2 * j] > 0, zero, never)
    scores = jnp.concatenate(
        [
            scores[:BLOCK] + root_off,
            scores[BLOCK : 2 * BLOCK] + own_off,
            scores[2 * BLOCK : 3 * BLOCK] + prev_off,
            scores[3 * BLOCK :] + rand_off,
        ],
        axis=0,
    )
    top = jnp.max(scores, axis=0, keepdims=True)
    weights = jnp.exp2(scores - top)
    total = jnp.sum(weights, axis=0, keepdims=True)
    probs = (weights * (1.0 / total)).astype(jnp.bfloat16)
    att_t = lax.dot_general(
        values, probs, (((0,), (0,)), ((), ())), preferred_element_type=jnp.float32
    ).astype(jnp.bfloat16)
    delta = jnp.sum(
        att_t.astype(jnp.float32) * up_t.astype(jnp.float32), axis=0, keepdims=True
    )
    dprob = lax.dot_general(
        values, up_t, (((1,), (0,)), ((), ())), preferred_element_type=jnp.float32
    )
    dscore = (probs.astype(jnp.float32) * (dprob - delta)).astype(jnp.bfloat16)
    dq_t = lax.dot_general(
        keys, dscore, (((0,), (0,)), ((), ())), preferred_element_type=jnp.float32
    )
    dq = (dq_t * scale).astype(jnp.bfloat16).T
    att = att_t.T
    for r in range(groups):
        att_ref[:, r * HEAD_SIZE : (r + 1) * HEAD_SIZE] = att[r * BLOCK : (r + 1) * BLOCK]
        dq_ref[:, r * HEAD_SIZE : (r + 1) * HEAD_SIZE] = dq[r * BLOCK : (r + 1) * BLOCK]
    dkey = scale * jnp.dot(dscore, q, preferred_element_type=jnp.float32)
    dvalue = jnp.dot(probs, up, preferred_element_type=jnp.float32)
    g_own[0, 0] = dkey[BLOCK : 2 * BLOCK]
    g_own[0, 1] = dvalue[BLOCK : 2 * BLOCK]
    g_prev[0, 0] = dkey[2 * BLOCK : 3 * BLOCK]
    g_prev[0, 1] = dvalue[2 * BLOCK : 3 * BLOCK]
    g_rand[0, 0] = dkey[3 * BLOCK :].astype(jnp.bfloat16)
    g_rand[0, 1] = dvalue[3 * BLOCK :].astype(jnp.bfloat16)

    @pl.when(j == 0)
    def _():
        g_root[...] = jnp.zeros_like(g_root)

    g_root[0] += dkey[:BLOCK]
    g_root[1] += dvalue[:BLOCK]


def attention(info, queries, upstream, own, edge, root, rand, earlier, chunk, chunk_heads):
    blocks = own.shape[0]
    width = chunk_heads * HEAD_SIZE
    groups = queries.shape[1] // own.shape[3]
    wide = groups * HEAD_SIZE
    start = chunk * chunk_heads
    token_spec = pl.BlockSpec((BLOCK, wide), lambda g, j, _: (j, start + g))
    set_shape = (1, 2, BLOCK, HEAD_SIZE)
    in_specs = [
        token_spec,
        token_spec,
        pl.BlockSpec(set_shape, lambda g, j, _: (j, 0, 0, start + g)),
        pl.BlockSpec(set_shape, lambda g, j, _: (jnp.maximum(j - 1, 0), 0, 0, start + g)),
        pl.BlockSpec(set_shape, lambda g, j, _: (0, 0, 0, start + g)),
        pl.BlockSpec(set_shape, lambda g, j, _: (0, 0, 0, start + g)),
        pl.BlockSpec(set_shape, lambda g, j, _: (j, 0, 0, g)),
    ]
    operands = [queries, upstream, own, own, edge, root, rand]
    aliases = {}
    if earlier is not None:
        in_specs += [pl.BlockSpec(memory_space=pl.ANY)] * 2
        operands += list(earlier)
        aliases = {8: 0, 9: 1}
    by_block = pl.BlockSpec(set_shape, lambda g, j, _: (j, 0, 0, g))
    set_array = (blocks, 2, BLOCK, width)
    elements = blocks * chunk_heads * groups * BLOCK * 4 * BLOCK
    return pl.pallas_call(
        functools.partial(attention_kernel, groups=groups, aliased=earlier is not None),
        grid_spec=pltpu.PrefetchScalarGridSpec(
            num_scalar_prefetch=1,
            grid=(chunk_heads, blocks),
            in_specs=in_specs,
            out_specs=[
                token_spec,
                token_spec,
                by_block,
                by_block,
                by_block,
                pl.BlockSpec((2, BLOCK, HEAD_SIZE), lambda g, j, _: (0, 0, g)),
            ],
        ),
        out_shape=[
            jax.ShapeDtypeStruct(queries.shape, jnp.bfloat16),
            jax.ShapeDtypeStruct(queries.shape, jnp.bfloat16),
            jax.ShapeDtypeStruct(set_array, jnp.float32),
            jax.ShapeDtypeStruct(set_array, jnp.float32),
            jax.ShapeDtypeStruct(set_array, jnp.bfloat16),
            jax.ShapeDtypeStruct((2, BLOCK, width), jnp.float32),
        ],
        input_output_aliases=aliases,
        cost_estimate=pl.CostEstimate(
            flops=12 * elements * HEAD_SIZE,
            transcendentals=elements,
            bytes_accessed=blocks * chunk_heads * wide * BLOCK * 8,
        ),
        compiler_params=pltpu.CompilerParams(vmem_limit_bytes=40 * 1024 * 1024),
        name="attention",
    )(info, *operands)


def place_kernel(index, own_ref, near_ref, far_ref, out_ref, total):
    slots = own_ref.shape[0]
    count = out_ref.shape[0]
    total[...] = jnp.zeros_like(total)
    for part, ref in enumerate((own_ref, near_ref, far_ref)):
        for n in range(slots):
            at = index[part * slots + n]
            inside = jnp.logical_and(at >= 0, at < count)

            @pl.when(inside)
            def _(at=at, ref=ref, n=n):
                total[jnp.clip(at, 0, count - 1)] += ref[n].astype(jnp.float32)

    out_ref[...] = total[...].astype(jnp.bfloat16)


def place(index, own, near, far, count):
    slots, _, _, width = own.shape
    tile = 128
    spec = pl.BlockSpec((slots, 2, BLOCK, tile), lambda g, _: (0, 0, 0, g))
    return pl.pallas_call(
        place_kernel,
        grid_spec=pltpu.PrefetchScalarGridSpec(
            num_scalar_prefetch=1,
            grid=(width // tile,),
            in_specs=[spec] * 3,
            out_specs=pl.BlockSpec((count, 2, BLOCK, tile), lambda g, _: (0, 0, 0, g)),
            scratch_shapes=[pltpu.VMEM((count, 2, BLOCK, tile), jnp.float32)],
        ),
        out_shape=jax.ShapeDtypeStruct((count, 2, BLOCK, width), jnp.bfloat16),
        cost_estimate=pl.CostEstimate(
            flops=count * 2 * BLOCK * width,
            transcendentals=0,
            bytes_accessed=(3 * slots + count) * 2 * BLOCK * width * 2,
        ),
        name="place",
    )(index, own, near, far)


def local(queries, key_rows, value_rows, upstream, ancestors):
    tokens, width = key_rows.shape
    blocks = tokens // BLOCK
    shard_blocks = ancestors.shape[0]
    both = ("seq", "head")
    shard, part = lax.axis_index("seq"), lax.axis_index("head")
    origin = shard * shard_blocks
    mine = lax.dynamic_slice_in_dim(ancestors, part * blocks, blocks, 0)
    first_entry, last_entry = mine[:, 0], mine[:, 1]
    use_prev = first_entry >= 0
    use_rand = (last_entry >= 0) & (last_entry != first_entry)
    info = jnp.concatenate(
        [
            (origin + part * blocks)[None].astype(jnp.int32),
            jnp.stack([use_prev, use_rand], 1).reshape(-1).astype(jnp.int32),
        ]
    )
    wanted_near = shifted(last_entry, "seq", -1) - origin
    wanted_far = shifted(last_entry, "seq", -2) - origin
    wanted_own = last_entry - origin
    length = lax.axis_size("seq")
    wanted_near = jnp.where(shard + 1 < length, wanted_near, -1)
    wanted_far = jnp.where(shard + 2 < length, wanted_far, -1)
    wanted = jnp.concatenate([wanted_own, wanted_near, wanted_far]).astype(jnp.int32)

    own = jnp.stack(
        [key_rows.reshape(blocks, BLOCK, width), value_rows.reshape(blocks, BLOCK, width)], 1
    )
    chunk_heads = width // HEAD_SIZE // CHUNKS
    chunk_width = chunk_heads * HEAD_SIZE
    is_first = (shard == 0) & (part == 0)
    edge = shifted(own[-1:], both, 1)
    root = jnp.where(is_first, own[:1], jnp.zeros_like(own[:1]))
    root = spread_from_first(spread_from_first(root, "head"), "seq")

    def at(x, index):
        return jnp.take(x, jnp.clip(index, 0, shard_blocks - 1), axis=0)

    rands = []
    back = shard - last_entry // shard_blocks
    for c in range(CHUNKS):
        piece = own[..., c * chunk_width : (c + 1) * chunk_width]
        whole = lax.all_gather(piece, "head", axis=0, tiled=True)
        near = shifted(at(whole, wanted_near), "seq", 1)
        far = shifted(at(whole, wanted_far), "seq", 2)
        pick = back[:, None, None, None]
        rands.append(
            jnp.where(pick == 0, at(whole, wanted_own), jnp.where(pick == 1, near, far))
        )
    outs = None
    key_grads, value_grads = [], []
    for c in range(CHUNKS):
        attended, query_grad, g_own, g_prev, g_rand, g_root = attention(
            info, queries, upstream, own, edge, root, rands[c], outs, c, chunk_heads
        )
        outs = (attended, query_grad)
        near = shifted(g_rand, "seq", -1)
        far = shifted(g_rand, "seq", -2)
        placed = place(wanted, g_rand, near, far, shard_blocks)
        summed = lax.psum_scatter(placed, "head", scatter_dimension=0, tiled=True)
        g_root = sum_to_first(sum_to_first(g_root, "seq"), "head")
        g_edge = shifted(g_prev[:1].astype(jnp.bfloat16), both, -1).astype(jnp.float32)
        total = g_own + summed.astype(jnp.float32)
        total = total + jnp.concatenate([g_prev[1:], g_edge], 0)
        head_of_row = jnp.where(is_first, g_root, 0.0)
        total = jnp.concatenate([total[:1] + head_of_row[None], total[1:]], 0)
        total = total.astype(jnp.bfloat16)
        key_grads.append(total[:, 0].reshape(tokens, chunk_width))
        value_grads.append(total[:, 1].reshape(tokens, chunk_width))
    return (
        outs[0],
        outs[1],
        jnp.concatenate(key_grads, 1),
        jnp.concatenate(value_grads, 1),
    )


def solution(mesh):
    tokens = P(("seq", "head"), None)
    return jax.shard_map(
        local,
        mesh=mesh,
        in_specs=(tokens, tokens, tokens, tokens, P("seq", None)),
        out_specs=(tokens, tokens, tokens, tokens),
        check_vma=False,
    )
```

time: 660 us -> 375 us (0.57); the launches traced: 652 us -> 374 us
  matrix products: 113 us -> 0 us
  waiting for transfers between devices: 316 us -> 214 us
  local copies, waits for them, and re-layouts: 114 us -> 32.4 us
  Pallas kernels: 0 us -> 46 us
  other arithmetic: 35.4 us -> 16.5 us
  starting transfers between devices: 58.5 us -> 50.9 us
    all_to_all x8 -> x0, waiting for transfers between devices: 254 us -> none  [the longest x1 78.4 us: local(): lax.all_to_all(attended_heads.reshape(tokens, -1), 'head', split_axis=0,...]
    ppermute x8 -> x28, waiting for transfers between devices: 21.2 us -> 147 us  [the longest x10 54.9 us: sum_to_first(): x = x + lax.ppermute(x, axis, pairs)]
    dot_general x19 -> x0, matrix products: 113 us -> none  [the longest x4 29.2 us: block_scores(): jnp.einsum('bqkgd,bskd->bkgqs', query_blocks, key_heads, preferred_elemen...]
    all_gather x0 -> x2, waiting for transfers between devices: none -> 66.2 us  [local(): whole = lax.all_gather(piece, 'head', axis=0, tiled=True)]
    pallas_call x0 -> x4, Pallas kernels: none -> 46 us  [the longest x2 36 us: attention(): pl.pallas_call(functools.partial(attention_kernel, groups=groups, aliased...]
    all_to_all x10 -> x0, local copies, waits for them, and re-layouts: 42 us -> none  [the longest x2 13.5 us: local(): lax.all_to_all(query_local, 'head', split_axis=0, concat_axis=1, tiled=True)]
    psum x2 -> x0, waiting for transfers between devices: 40.7 us -> none  [the longest x1 40.7 us: local(): lax.psum((key_parts[0].reshape(ROOT, kv_width), value_parts[0].reshape(RO...]
    all_to_all x8 -> x0, starting transfers between devices: 39.4 us -> none  [the longest x1 6.32 us: local(): lax.all_to_all(key_rows, 'head', split_axis=1, concat_axis=0, tiled=True)]
  transfers between devices with their start and end apart: 18 -> 32, of which waited for: 10 -> 19; matrix products, arithmetic and copies ran while one was open for 27% -> 7% of each run, Pallas kernels for 0% -> 6%
where the time goes in v1:
time: 375 us; the launch traced here: 374 us
  waiting for transfers between devices  214 us (57%)
  starting transfers between devices  50.9 us (14%)
  Pallas kernels  46 us (12%)
  local copies, waits for them, and re-layouts  32.4 us (9%)
  other arithmetic  16.5 us (4%)
  between operations  14.5 us (4%)
    all_gather x2, waiting for transfers between devices, local(): whole = lax.all_gather(piece, 'head', axis=0, tiled=True)  66.2 us
    ppermute x10, waiting for transfers between devices, sum_to_first(): x = x + lax.ppermute(x, axis, pairs)  54.9 us
    ppermute x5, waiting for transfers between devices, spread_from_first(): x = x + lax.ppermute(x, axis, pairs)  48 us
    ppermute x13, waiting for transfers between devices, shifted(): return lax.ppermute(x, axis, pairs)  43.9 us
    pallas_call x2, Pallas kernels, attention(): pl.pallas_call(functools.partial(attention_kernel, groups=groups, aliased...  36 us
    ppermute x13, starting transfers between devices, shifted(): return lax.ppermute(x, axis, pairs)  25.2 us
    unnamed x54, local copies, waits for them, and re-layouts  17.9 us
    ppermute x10, starting transfers between devices, sum_to_first(): x = x + lax.ppermute(x, axis, pairs)  13 us
  transfers between devices with their start and end apart: 32, of which 19 were waited for; matrix products, arithmetic and copies ran while one was open for 7% of the time, Pallas kernels for 6%

profile of v1, /device:TPU:0, one launch (start us, length us, event | category | flops | bytes accessed | tf_op | source)
XLA Modules:
  0.0 374.1 jit_solution(3117581053590586017)
XLA Ops:
  7.2 2.3 fusion.1
  13.9 4.9 %collective-permute-start.1 = (bf16[1,2,64,1024]{3,2,1,0:T(8,128)(2,1)S(1)}, bf16[1,2,64,1024]{3,2,1,0:T(8,128)(2,1)S(1)}, u32[]{:S(2)}, u32[]{:S(2)}) collective-permute-start(bf16[1,2,64,1024]{3,2,1,0:T(8,128)(2,1)S(1)} %get-tuple-element.42), channel_id=1, source_target_pairs={{0,1},{4,5},{8,9},{12,13},{16,17},{20,21},{24,25},{28,29}} | collective-permute-start | bytes 786440 | tf_op jit(solution)/shard_map/ppermute | solution.py:28
  18.9 10.6 %collective-permute-done.1 = bf16[1,2,64,1024]{3,2,1,0:T(8,128)(2,1)S(1)} collective-permute-done((bf16[1,2,64,1024]{3,2,1,0:T(8,128)(2,1)S(1)}, bf16[1,2,64,1024]{3,2,1,0:T(8,128)(2,1)S(1)}, u32[]{:S(2)}, u32[]{:S(2)}) %collective-permute-start.1) | collective-permute-done | bytes 262176 | tf_op jit(solution)/shard_map/ppermute | solution.py:28
  30.9 12.2 %collective-permute-done.2 = bf16[1,2,64,1024]{3,2,1,0:T(8,128)(2,1)S(1)} collective-permute-done((bf16[1,2,64,1024]{3,2,1,0:T(8,128)(2,1)S(1)}, bf16[1,2,64,1024]{3,2,1,0:T(8,128)(2,1)S(1)}, u32[]{:S(2)}, u32[]{:S(2)}) %collective-permute-start.2) | collective-permute-done | bytes 262176 | tf_op jit(solution)/shard_map/ppermute | solution.py:28
  46.4 3.1 collective-permute-start.4
  49.4 15.9 %all-gather.3.cloned.1.call-done = bf16[16,2,64,512]{3,2,1,0:T(8,128)(2,1)} async-done(((bf16[4,2,64,512]{3,2,1,0:T(8,128)(2,1)}), bf16[16,2,64,512]{3,2,1,0:T(8,128)(2,1)}) %all-gather.3.cloned.1.call-update) | async-done | bytes 2097168 | tf_op jit(solution)/shard_map/all_gather | solution.py:266
  67.5 50.3 %all-gather.5.cloned.1.call-done = bf16[16,2,64,512]{3,2,1,0:T(8,128)(2,1)} async-done(((bf16[4,2,64,512]{3,2,1,0:T(8,128)(2,1)}), bf16[16,2,64,512]{3,2,1,0:T(8,128)(2,1)}) %all-gather.5.cloned.1.call-update) | async-done | bytes 2097168 | tf_op jit(solution)/shard_map/all_gather | solution.py:266
  122.9 4.4 %collective-permute-start.7 = (bf16[4,2,64,512]{3,2,1,0:T(8,128)(2,1)}, bf16[4,2,64,512]{3,2,1,0:T(8,128)(2,1)}, u32[]{:S(2)}, u32[]{:S(2)}) collective-permute-start(bf16[4,2,64,512]{3,2,1,0:T(8,128)(2,1)} %get-tuple-element.58), channel_id=1, source_target_pairs={{0,4},{4,8},{8,12},{12,16},{16,20},{20,24},{24,28},{1,5},{5,9},{9,... | collective-permute-start | bytes 1572872 | tf_op jit(solution)/shard_map/ppermute | solution.py:20
  129.5 2.2 gather_fusion.5
  132.8 3.4 collective-permute-start.11
  136.2 3.3 collective-permute-start.9
  141.3 24.1 %collective-permute-done.5 = bf16[1,2,64,1024]{3,2,1,0:T(8,128)(2,1)S(1)} collective-permute-done((bf16[1,2,64,1024]{3,2,1,0:T(8,128)(2,1)S(1)}, bf16[1,2,64,1024]{3,2,1,0:T(8,128)(2,1)S(1)}, u32[]{:S(2)}, u32[]{:S(2)}) %collective-permute-start.5) | collective-permute-done | bytes 262176 | tf_op jit(solution)/shard_map/ppermute | solution.py:28
  169.5 2.2 gather_fusion.3
  175.3 2.2 copy-done.3
  178.4 17.9 %attention.2 = (bf16[256,8192]{1,0:T(8,128)(2,1)}, bf16[256,8192]{1,0:T(8,128)(2,1)}, f32[4,2,64,512]{3,2,1,0:T(8,128)S(1)}, f32[4,2,64,512]{3,2,1,0:T(8,128)S(1...) custom-call(s32[9]{0:T(128)S(1)} %pad_add_fusion.info, bf16[256,8192]{1,0:T(8,128)(2,1)S(1)} %copy-done.1, ...), custom_call_target="tpu_custom_call" | custom-call | flops 3221225472 | bytes 8388608 | tf_op jit(solution)/shard_map/attention/pallas_call | solution.py:151
  201.2 13.1 %collective-permute-done.13.far_ref = bf16[4,2,64,512]{3,2,1,0:T(8,128)(2,1)S(1)} collective-permute-done((bf16[4,2,64,512]{3,2,1,0:T(8,128)(2,1)S(1)}, bf16[4,2,64,512]{3,2,1,0:T(8,128)(2,1)S(1)}, u32[]{:S(2)}, u32[]{:S(2)}) %collective-permute-start.13) | collective-permute-done | bytes 524320 | tf_op jit(solution)/shard_map/ppermute | solution.py:20
  215.1 5.0 %place.2 = bf16[16,2,64,512]{3,2,1,0:T(8,128)(2,1)} custom-call(s32[12]{0:T(128)} %pad_add_fusion.1.index, bf16[4,2,64,512]{3,2,1,0:T(8,128)(2,1)} %copy-done.11, bf16[4,2,64,512]{3,2,1,0:T(8,128)(2,1)} %collective-permute-done.12.near_ref, bf16[4,2,64,512]{3,2,1,0:T(8,128)(2,1)} %copy-done.24), custom_call_target="tpu_custom_call" | custom-call | flops 1048576 | bytes 3670016 | tf_op jit(solution)/shard_map/place/pallas_call | solution.py:205
  220.2 2.2 copy-done.2
  222.4 2.2 copy-done.4
  225.5 18.1 %attention.3 = (bf16[256,8192]{1,0:T(8,128)(2,1)}, bf16[256,8192]{1,0:T(8,128)(2,1)}, f32[4,2,64,512]{3,2,1,0:T(8,128)S(1)}, f32[4,2,64,512]{3,2,1,0:T(8,128)S(1...) custom-call(s32[9]{0:T(128)S(1)} %pad_add_fusion.info, ...), custom_call_target="tpu_custom_call", output_to_operand_aliasing={{0}: (8, {}), {1}: (9, {})} | custom-call | flops 3221225472 | bytes 8388608 | tf_op jit(solution)/shard_map/attention/pallas_call | solution.py:151
  249.1 14.2 %collective-permute-done.21.far_ref = bf16[4,2,64,512]{3,2,1,0:T(8,128)(2,1)S(1)} collective-permute-done((bf16[4,2,64,512]{3,2,1,0:T(8,128)(2,1)S(1)}, bf16[4,2,64,512]{3,2,1,0:T(8,128)(2,1)S(1)}, u32[]{:S(2)}, u32[]{:S(2)}) %collective-permute-start.21) | collective-permute-done | bytes 524320 | tf_op jit(solution)/shard_map/ppermute | solution.py:20
  264.9 5.0 %place.3 = bf16[16,2,64,512]{3,2,1,0:T(8,128)(2,1)} custom-call(s32[12]{0:T(128)} %pad_add_fusion.1.index, bf16[4,2,64,512]{3,2,1,0:T(8,128)(2,1)} %copy-done.12, bf16[4,2,64,512]{3,2,1,0:T(8,128)(2,1)} %copy-done.26, bf16[4,2,64,512]{3,2,1,0:T(8,128)(2,1)} %copy-done.25), custom_call_target="tpu_custom_call" | custom-call | flops 1048576 | bytes 3670016 | tf_op jit(solution)/shard_map/place/pallas_call | solution.py:205
  272.5 12.6 %collective-permute-done.15 = f32[2,64,512]{2,1,0:T(8,128)S(1)} collective-permute-done((f32[2,64,512]{2,1,0:T(8,128)S(1)}, f32[2,64,512]{2,1,0:T(8,128)S(1)}, u32[]{:S(2)}, u32[]{:S(2)}) %collective-permute-start.15) | collective-permute-done | bytes 262176 | tf_op jit(solution)/shard_map/ppermute | solution.py:41
  286.6 4.1 %collective-permute-done.23 = f32[2,64,512]{2,1,0:T(8,128)S(1)} collective-permute-done((f32[2,64,512]{2,1,0:T(8,128)S(1)}, f32[2,64,512]{2,1,0:T(8,128)S(1)}, u32[]{:S(2)}, u32[]{:S(2)}) %collective-permute-start.23) | collective-permute-done | bytes 262176 | tf_op jit(solution)/shard_map/ppermute | solution.py:41
  292.0 2.5 collective-permute-done.16
  295.9 5.7 %collective-permute-done.24 = f32[2,64,512]{2,1,0:T(8,128)S(1)} collective-permute-done((f32[2,64,512]{2,1,0:T(8,128)S(1)}, f32[2,64,512]{2,1,0:T(8,128)S(1)}, u32[]{:S(2)}, u32[]{:S(2)}) %collective-permute-start.24) | collective-permute-done | bytes 262176 | tf_op jit(solution)/shard_map/ppermute | solution.py:41
  310.2 10.9 %collective-permute-done.14 = bf16[1,2,64,512]{3,2,1,0:T(8,128)(2,1)S(1)} collective-permute-done((bf16[1,2,64,512]{3,2,1,0:T(8,128)(2,1)S(1)}, bf16[1,2,64,512]{3,2,1,0:T(8,128)(2,1)S(1)}, u32[]{:S(2)}, u32[]{:S(2)}) %collective-permute-start.14) | collective-permute-done | bytes 131104 | tf_op jit(solution)/shard_map/ppermute | solution.py:20
  321.1 5.8 %collective-permute-done.22 = bf16[1,2,64,512]{3,2,1,0:T(8,128)(2,1)S(1)} collective-permute-done((bf16[1,2,64,512]{3,2,1,0:T(8,128)(2,1)S(1)}, bf16[1,2,64,512]{3,2,1,0:T(8,128)(2,1)S(1)}, u32[]{:S(2)}, u32[]{:S(2)}) %collective-permute-start.22) | collective-permute-done | bytes 131104 | tf_op jit(solution)/shard_map/ppermute | solution.py:20
  326.8 11.1 %collective-permute-done.18 = f32[2,64,512]{2,1,0:T(8,128)S(1)} collective-permute-done((f32[2,64,512]{2,1,0:T(8,128)S(1)}, f32[2,64,512]{2,1,0:T(8,128)S(1)}, u32[]{:S(2)}, u32[]{:S(2)}) %collective-permute-start.18) | collective-permute-done | bytes 262176 | tf_op jit(solution)/shard_map/ppermute | solution.py:41
  339.9 3.7 collective-permute-done.26
  349.8 9.4 %collective-permute-done.19 = f32[2,64,512]{2,1,0:T(8,128)} collective-permute-done((f32[2,64,512]{2,1,0:T(8,128)}, f32[2,64,512]{2,1,0:T(8,128)}, u32[]{:S(2)}, u32[]{:S(2)}) %collective-permute-start.19) | collective-permute-done | bytes 262176 | tf_op jit(solution)/shard_map/ppermute | solution.py:41
  359.2 5.1 %collective-permute-done.27 = f32[2,64,512]{2,1,0:T(8,128)} collective-permute-done((f32[2,64,512]{2,1,0:T(8,128)}, f32[2,64,512]{2,1,0:T(8,128)}, u32[]{:S(2)}, u32[]{:S(2)}) %collective-permute-start.27) | collective-permute-done | bytes 262176 | tf_op jit(solution)/shard_map/ppermute | solution.py:41
  (149 shorter events, 70.0 us)
Async XLA Ops:
  7.2 58.1 %all-gather.3.cloned.1.call-start = ((), (), s32[]{:S(2)}) async-start(), calls=%async_computation.2 | async-start | bytes 2621440 | tf_op jit(solution)/shard_map/all_gather | solution.py:266
  9.6 108.2 %all-gather.5.cloned.1.call-start = ((), (), s32[]{:S(2)}) async-start(), calls=%async_computation.3 | async-start | bytes 2621440 | tf_op jit(solution)/shard_map/all_gather | solution.py:266
  10.4 335.3 %reduce-scatter.3.cloned.1.call-start = ((), (), s32[]{:S(2)}) async-start(), calls=%async_computation.4 | async-start | bytes 2621440 | tf_op jit(solution)/shard_map/reduce_scatter | solution.py:283
  10.5 20.4 %collective-permute-start.6 = (s32[4]{0:T(128)S(1)}, s32[4]{0:T(128)S(1)}, u32[]{:S(2)}, u32[]{:S(2)}) collective-permute-start(s32[4]{0:T(128)S(1)} %slice_bitcast_fusion), channel_id=1, source_target_pairs={{4,0},{8,4},{12,8},{16,12},{20,16},{24,20},{28,24},{5,1},{9,5},{13... | collective-permute-start | bytes 56 | tf_op jit(solution)/shard_map/ppermute | solution.py:20
  11.8 33.4 %collective-permute-start.8 = (s32[4]{0:T(128)S(1)}, s32[4]{0:T(128)S(1)}, u32[]{:S(2)}, u32[]{:S(2)}) collective-permute-start(s32[4]{0:T(128)S(1)} %slice_bitcast_fusion), channel_id=1, source_target_pairs={{8,0},{12,4},{16,8},{20,12},{24,16},{28,20},{9,1},{13,5},{17,9},{2... | collective-permute-start | bytes 56 | tf_op jit(solution)/shard_map/ppermute | solution.py:20
  13.9 15.6 %collective-permute-start.1 = (bf16[1,2,64,1024]{3,2,1,0:T(8,128)(2,1)S(1)}, bf16[1,2,64,1024]{3,2,1,0:T(8,128)(2,1)S(1)}, u32[]{:S(2)}, u32[]{:S(2)}) collective-permute-start(bf16[1,2,64,1024]{3,2,1,0:T(8,128)(2,1)S(1)} %get-tuple-element.42), channel_id=1, source_target_pairs={{0,1},{4,5},{8,9},{12,13},{16,17},{20,21},{24,25},{28,29}} | collective-permute-start | bytes 786440 | tf_op jit(solution)/shard_map/ppermute | solution.py:28
  29.6 13.6 %collective-permute-start.2 = (bf16[1,2,64,1024]{3,2,1,0:T(8,128)(2,1)S(1)}, bf16[1,2,64,1024]{3,2,1,0:T(8,128)(2,1)S(1)}, u32[]{:S(2)}, u32[]{:S(2)}) collective-permute-start(bf16[1,2,64,1024]{3,2,1,0:T(8,128)(2,1)S(1)} %add.92), channel_id=1, source_target_pairs={{0,2},{1,3},{4,6},{5,7},{8,10},{9,11},{12,14},{13,15},{16,18},{17,... | collective-permute-start | bytes 786440 | tf_op jit(solution)/shard_map/ppermute | solution.py:28
  43.2 3.1 collective-permute-start.3
  46.4 93.5 %collective-permute-start.4 = (bf16[1,2,64,1024]{3,2,1,0:T(8,128)(2,1)S(1)}, bf16[1,2,64,1024]{3,2,1,0:T(8,128)(2,1)S(1)}, u32[]{:S(2)}, u32[]{:S(2)}) collective-permute-start(bf16[1,2,64,1024]{3,2,1,0:T(8,128)(2,1)S(1)} %add.94), channel_id=1, source_target_pairs={{0,8},{4,12},{1,9},{5,13},{2,10},{6,14},{3,11},{7,15}} | collective-permute-start | bytes 786440 | tf_op jit(solution)/shard_map/ppermute | solution.py:28
  121.1 50.5 %collective-permute-start.10 = (bf16[4,2,64,512]{3,2,1,0:T(8,128)(2,1)}, bf16[4,2,64,512]{3,2,1,0:T(8,128)(2,1)S(1)}, u32[]{:S(2)}, u32[]{:S(2)}) collective-permute-start(bf16[4,2,64,512]{3,2,1,0:T(8,128)(2,1)} %get-tuple-element.57), channel_id=1, source_target_pairs={{0,4},{4,8},{8,12},{12,16},{16,20},{20,24},{24,28},{1,5},{5,9},{9,... | collective-permute-start | bytes 1572872 | tf_op jit(solution)/shard_map/ppermute | solution.py:20
  122.9 48.8 %collective-permute-start.7 = (bf16[4,2,64,512]{3,2,1,0:T(8,128)(2,1)}, bf16[4,2,64,512]{3,2,1,0:T(8,128)(2,1)}, u32[]{:S(2)}, u32[]{:S(2)}) collective-permute-start(bf16[4,2,64,512]{3,2,1,0:T(8,128)(2,1)} %get-tuple-element.58), channel_id=1, source_target_pairs={{0,4},{4,8},{8,12},{12,16},{16,20},{20,24},{24,28},{1,5},{5,9},{9,... | collective-permute-start | bytes 1572872 | tf_op jit(solution)/shard_map/ppermute | solution.py:20
  132.8 38.9 %collective-permute-start.11 = (bf16[4,2,64,512]{3,2,1,0:T(8,128)(2,1)}, bf16[4,2,64,512]{3,2,1,0:T(8,128)(2,1)}, u32[]{:S(2)}, u32[]{:S(2)}) collective-permute-start(bf16[4,2,64,512]{3,2,1,0:T(8,128)(2,1)} %get-tuple-element.55), channel_id=1, source_target_pairs={{0,8},{4,12},{8,16},{12,20},{16,24},{20,28},{1,9},{5,13},{9,17},{1... | collective-permute-start | bytes 1572872 | tf_op jit(solution)/shard_map/ppermute | solution.py:20
  136.2 35.5 %collective-permute-start.9 = (bf16[4,2,64,512]{3,2,1,0:T(8,128)(2,1)}, bf16[4,2,64,512]{3,2,1,0:T(8,128)(2,1)}, u32[]{:S(2)}, u32[]{:S(2)}) collective-permute-start(bf16[4,2,64,512]{3,2,1,0:T(8,128)(2,1)} %get-tuple-element.56), channel_id=1, source_target_pairs={{0,8},{4,12},{8,16},{12,20},{16,24},{20,28},{1,9},{5,13},{9,17},{1... | collective-permute-start | bytes 1572872 | tf_op jit(solution)/shard_map/ppermute | solution.py:20
  139.9 25.5 %collective-permute-start.5 = (bf16[1,2,64,1024]{3,2,1,0:T(8,128)(2,1)S(1)}, bf16[1,2,64,1024]{3,2,1,0:T(8,128)(2,1)S(1)}, u32[]{:S(2)}, u32[]{:S(2)}) collective-permute-start(bf16[1,2,64,1024]{3,2,1,0:T(8,128)(2,1)S(1)} %add.95), channel_id=1, source_target_pairs={{0,16},{4,20},{8,24},{12,28},{1,17},{5,21},{9,25},{13,29},{2,18},{... | collective-permute-start | bytes 786440 | tf_op jit(solution)/shard_map/ppermute | solution.py:28
  165.4 9.0 %collective-permute-start = (bf16[1,2,64,1024]{3,2,1,0:T(8,128)(2,1)}, bf16[1,2,64,1024]{3,2,1,0:T(8,128)(2,1)S(1)}, u32[]{:S(2)}, u32[]{:S(2)}) collective-permute-start(bf16[1,2,64,1024]{3,2,1,0:T(8,128)(2,1)} %get-tuple-element.43), channel_id=1, source_target_pairs={{0,1},{1,2},{2,3},{3,4},{4,5},{5,6},{6,7},{7,8},{8,9},{9,10},{10,1... | collective-permute-start | bytes 786440 | tf_op jit(solution)/shard_map/ppermute | solution.py:20
  198.0 16.3 %collective-permute-start.13 = (bf16[4,2,64,512]{3,2,1,0:T(8,128)(2,1)S(1)}, bf16[4,2,64,512]{3,2,1,0:T(8,128)(2,1)S(1)}, u32[]{:S(2)}, u32[]{:S(2)}) collective-permute-start(bf16[4,2,64,512]{3,2,1,0:T(8,128)(2,1)S(1)} %get-tuple-element.22.own_ref), channel_id=1, source_target_pairs={{8,0},{12,4},{16,8},{20,12},{24,16},{28,20},{9,1},{13,5},{17,9},{2... | collective-permute-start | bytes 1572872 | tf_op jit(solution)/shard_map/ppermute | solution.py:20
  199.3 15.8 %collective-permute-start.12 = (bf16[4,2,64,512]{3,2,1,0:T(8,128)(2,1)S(1)}, bf16[4,2,64,512]{3,2,1,0:T(8,128)(2,1)}, u32[]{:S(2)}, u32[]{:S(2)}) collective-permute-start(bf16[4,2,64,512]{3,2,1,0:T(8,128)(2,1)S(1)} %get-tuple-element.22.own_ref), channel_id=1, source_target_pairs={{4,0},{8,4},{12,8},{16,12},{20,16},{24,20},{28,24},{5,1},{9,5},{13... | collective-permute-start | bytes 1572872 | tf_op jit(solution)/shard_map/ppermute | solution.py:20
  220.1 128.3 %reduce-scatter.5.cloned.1.call-start = ((), (), s32[]{:S(2)}) async-start(), calls=%async_computation.5 | async-start | bytes 2621440 | tf_op jit(solution)/shard_map/reduce_scatter | solution.py:283
  246.3 16.9 %collective-permute-start.21 = (bf16[4,2,64,512]{3,2,1,0:T(8,128)(2,1)S(1)}, bf16[4,2,64,512]{3,2,1,0:T(8,128)(2,1)S(1)}, u32[]{:S(2)}, u32[]{:S(2)}) collective-permute-start(bf16[4,2,64,512]{3,2,1,0:T(8,128)(2,1)S(1)} %get-tuple-element.26.own_ref), channel_id=1, source_target_pairs={{8,0},{12,4},{16,8},{20,12},{24,16},{28,20},{9,1},{13,5},{17,9},{2... | collective-permute-start | bytes 1572872 | tf_op jit(solution)/shard_map/ppermute | solution.py:20
  247.8 15.5 %collective-permute-start.20 = (bf16[4,2,64,512]{3,2,1,0:T(8,128)(2,1)S(1)}, bf16[4,2,64,512]{3,2,1,0:T(8,128)(2,1)S(1)}, u32[]{:S(2)}, u32[]{:S(2)}) collective-permute-start(bf16[4,2,64,512]{3,2,1,0:T(8,128)(2,1)S(1)} %get-tuple-element.26.own_ref), channel_id=1, source_target_pairs={{4,0},{8,4},{12,8},{16,12},{20,16},{24,20},{28,24},{5,1},{9,5},{13... | collective-permute-start | bytes 1572872 | tf_op jit(solution)/shard_map/ppermute | solution.py:20
  269.9 15.2 %collective-permute-start.15 = (f32[2,64,512]{2,1,0:T(8,128)S(1)}, f32[2,64,512]{2,1,0:T(8,128)S(1)}, u32[]{:S(2)}, u32[]{:S(2)}) collective-permute-start(f32[2,64,512]{2,1,0:T(8,128)S(1)} %copy-done.17), channel_id=1, source_target_pairs={{16,0},{20,4},{24,8},{28,12},{17,1},{21,5},{25,9},{29,13},{18,2},{... | collective-permute-start | bytes 786440 | tf_op jit(solution)/shard_map/ppermute | solution.py:41
  271.2 19.5 %collective-permute-start.23 = (f32[2,64,512]{2,1,0:T(8,128)S(1)}, f32[2,64,512]{2,1,0:T(8,128)S(1)}, u32[]{:S(2)}, u32[]{:S(2)}) collective-permute-start(f32[2,64,512]{2,1,0:T(8,128)S(1)} %copy-done.19), channel_id=1, source_target_pairs={{16,0},{20,4},{24,8},{28,12},{17,1},{21,5},{25,9},{29,13},{18,2},{... | collective-permute-start | bytes 786440 | tf_op jit(solution)/shard_map/ppermute | solution.py:41
  285.1 9.4 %collective-permute-start.16 = (f32[2,64,512]{2,1,0:T(8,128)S(1)}, f32[2,64,512]{2,1,0:T(8,128)S(1)}, u32[]{:S(2)}, u32[]{:S(2)}) collective-permute-start(f32[2,64,512]{2,1,0:T(8,128)S(1)} %add.101), channel_id=1, source_target_pairs={{8,0},{12,4},{9,1},{13,5},{10,2},{14,6},{11,3},{15,7}} | collective-permute-start | bytes 786440 | tf_op jit(solution)/shard_map/ppermute | solution.py:41
  290.7 10.9 %collective-permute-start.24 = (f32[2,64,512]{2,1,0:T(8,128)S(1)}, f32[2,64,512]{2,1,0:T(8,128)S(1)}, u32[]{:S(2)}, u32[]{:S(2)}) collective-permute-start(f32[2,64,512]{2,1,0:T(8,128)S(1)} %add.109), channel_id=1, source_target_pairs={{8,0},{12,4},{9,1},{13,5},{10,2},{14,6},{11,3},{15,7}} | collective-permute-start | bytes 786440 | tf_op jit(solution)/shard_map/ppermute | solution.py:41
  294.6 8.4 %collective-permute-start.17 = (f32[2,64,512]{2,1,0:T(8,128)S(1)}, f32[2,64,512]{2,1,0:T(8,128)S(1)}, u32[]{:S(2)}, u32[]{:S(2)}) collective-permute-start(f32[2,64,512]{2,1,0:T(8,128)S(1)} %add.102), channel_id=1, source_target_pairs={{4,0},{5,1},{6,2},{7,3}} | collective-permute-start | bytes 786440 | tf_op jit(solution)/shard_map/ppermute | solution.py:41
  301.7 3.4 collective-permute-start.25
  303.0 34.9 %collective-permute-start.18 = (f32[2,64,512]{2,1,0:T(8,128)S(1)}, f32[2,64,512]{2,1,0:T(8,128)S(1)}, u32[]{:S(2)}, u32[]{:S(2)}) collective-permute-start(f32[2,64,512]{2,1,0:T(8,128)S(1)} %add.103), channel_id=1, source_target_pairs={{2,0},{3,1},{6,4},{7,5},{10,8},{11,9},{14,12},{15,13},{18,16},{19,... | collective-permute-start | bytes 786440 | tf_op jit(solution)/shard_map/ppermute | solution.py:41
  305.1 38.5 %collective-permute-start.26 = (f32[2,64,512]{2,1,0:T(8,128)S(1)}, f32[2,64,512]{2,1,0:T(8,128)S(1)}, u32[]{:S(2)}, u32[]{:S(2)}) collective-permute-start(f32[2,64,512]{2,1,0:T(8,128)S(1)} %add.111), channel_id=1, source_target_pairs={{2,0},{3,1},{6,4},{7,5},{10,8},{11,9},{14,12},{15,13},{18,16},{19,... | collective-permute-start | bytes 786440 | tf_op jit(solution)/shard_map/ppermute | solution.py:41
  306.5 14.6 %collective-permute-start.14 = (bf16[1,2,64,512]{3,2,1,0:T(8,128)(2,1)S(1)}, bf16[1,2,64,512]{3,2,1,0:T(8,128)(2,1)S(1)}, u32[]{:S(2)}, u32[]{:S(2)}) collective-permute-start(bf16[1,2,64,512]{3,2,1,0:T(8,128)(2,1)S(1)} %slice.165), channel_id=1, source_target_pairs={{1,0},{2,1},{3,2},{4,3},{5,4},{6,5},{7,6},{8,7},{9,8},{10,9},{11,1... | collective-permute-start | bytes 393224 | tf_op jit(solution)/shard_map/ppermute | solution.py:20
  307.8 19.0 %collective-permute-start.22 = (bf16[1,2,64,512]{3,2,1,0:T(8,128)(2,1)S(1)}, bf16[1,2,64,512]{3,2,1,0:T(8,128)(2,1)S(1)}, u32[]{:S(2)}, u32[]{:S(2)}) collective-permute-start(bf16[1,2,64,512]{3,2,1,0:T(8,128)(2,1)S(1)} %slice.164), channel_id=1, source_target_pairs={{1,0},{2,1},{3,2},{4,3},{5,4},{6,5},{7,6},{8,7},{9,8},{10,9},{11,1... | collective-permute-start | bytes 393224 | tf_op jit(solution)/shard_map/ppermute | solution.py:20
  338.6 20.6 %collective-permute-start.19 = (f32[2,64,512]{2,1,0:T(8,128)}, f32[2,64,512]{2,1,0:T(8,128)}, u32[]{:S(2)}, u32[]{:S(2)}) collective-permute-start(f32[2,64,512]{2,1,0:T(8,128)} %add.104), channel_id=1, source_target_pairs={{1,0},{5,4},{9,8},{13,12},{17,16},{21,20},{25,24},{29,28}} | collective-permute-start | bytes 786440 | tf_op jit(solution)/shard_map/ppermute | solution.py:41
  344.3 20.0 %collective-permute-start.27 = (f32[2,64,512]{2,1,0:T(8,128)}, f32[2,64,512]{2,1,0:T(8,128)}, u32[]{:S(2)}, u32[]{:S(2)}) collective-permute-start(f32[2,64,512]{2,1,0:T(8,128)} %add.112), channel_id=1, source_target_pairs={{1,0},{5,4},{9,8},{13,12},{17,16},{21,20},{25,24},{29,28}} | collective-permute-start | bytes 786440 | tf_op jit(solution)/shard_map/ppermute | solution.py:41
  (27 other events, 164.9 us)
Sparse Core Ops, SparseCore 0:
  10.2 55.0 all-gather.2
  67.4 50.3 all-gather.4
  220.2 49.3 reduce-scatter.2
  271.9 60.4 reduce-scatter.4

commit v2 on v1

--- a/solution.py
+++ b/solution.py
@@ -18,28 +18,6 @@
     length = lax.axis_size(axis)
     pairs = [(i, i + by) for i in range(length) if 0 <= i + by < length]
     return lax.ppermute(x, axis, pairs)
-
-
-def spread_from_first(x, axis):
-    length = lax.axis_size(axis)
-    step = 1
-    while step < length:
-        pairs = [(i, i + step) for i in range(step) if i + step < length]
-        x = x + lax.ppermute(x, axis, pairs)
-        step *= 2
-    return x
-
-
-def sum_to_first(x, axis):
-    length = lax.axis_size(axis)
-    step = 1
-    while step < length:
-        step *= 2
-    while step > 1:
-        step //= 2
-        pairs = [(i + step, i) for i in range(step) if i + step < length]
-        x = x + lax.ppermute(x, axis, pairs)
-    return x
 
 
 def attention_kernel(
@@ -137,7 +115,7 @@
         pl.BlockSpec(set_shape, lambda g, j, _: (jnp.maximum(j - 1, 0), 0, 0, start + g)),
         pl.BlockSpec(set_shape, lambda g, j, _: (0, 0, 0, start + g)),
         pl.BlockSpec(set_shape, lambda g, j, _: (0, 0, 0, start + g)),
-        pl.BlockSpec(set_shape, lambda g, j, _: (j, 0, 0, g)),
+        pl.BlockSpec(set_shape, lambda g, j, _: (j, 0, 0, start + g)),
     ]
     operands = [queries, upstream, own, own, edge, root, rand]
     aliases = {}
@@ -221,6 +199,370 @@
     )(index, own, near, far)
 
 
+PIECES = 4
+
+
+def tree_steps(length):
+    steps, step = [], 1
+    while step < length:
+        steps.append(step)
+        step *= 2
+    return steps
+
+
+def greet(head_steps, seq_steps, head_size, seq_size):
+    shard, part = lax.axis_index("seq"), lax.axis_index("head")
+    barrier = pltpu.get_barrier_semaphore()
+    count = 0
+    for axis, at, steps, length in (
+        ("head", part, head_steps, head_size),
+        ("seq", shard, seq_steps, seq_size),
+    ):
+        for step in steps:
+            for other in (lax.rem(at + step, length), lax.rem(at + length - step, length)):
+                pl.semaphore_signal(
+                    barrier, inc=1, device_id={axis: other}, device_id_type=pl.DeviceIdType.MESH
+                )
+                count += 1
+    pl.semaphore_wait(barrier, count)
+
+
+def send(source, target, send_sem, recv_sem, axis, other):
+    return pltpu.make_async_remote_copy(
+        src_ref=source,
+        dst_ref=target,
+        send_sem=send_sem,
+        recv_sem=recv_sem,
+        device_id={axis: other},
+        device_id_type=pl.DeviceIdType.MESH,
+    )
+
+
+def piece_of(c, width):
+    half = width * 2 // PIECES
+    return c // (PIECES // 2), pl.ds((c % (PIECES // 2)) * half, half)
+
+
+def gather_kernel(
+    head_size, seq_size, wanted, back, own, rand, root_out, *rest
+):
+    wholes, rest = rest[:PIECES], rest[PIECES:]
+    (root, stage_near, stage_far, in_near, in_far,
+     right_send, right_recv, left_send, left_recv, near_send, near_recv, far_send, far_recv,
+     root_send, root_recv) = rest
+    shard, part = lax.axis_index("seq"), lax.axis_index("head")
+    blocks, _, _, width = own.shape
+    count = wholes[0].shape[0]
+    head_steps, seq_steps = tree_steps(head_size), tree_steps(seq_size)
+    greet(head_steps, seq_steps, head_size, seq_size)
+    right = jnp.minimum(part + 1, head_size - 1)
+    left = jnp.maximum(part - 1, 0)
+    for c in range(PIECES):
+        kv, columns = piece_of(c, width)
+        wholes[c][pl.ds(part * blocks, blocks)] = own[:, kv, :, columns]
+
+    @pl.when(jnp.logical_and(shard == 0, part == 0))
+    def _():
+        root[...] = own[0]
+
+    def piece(p, c):
+        return wholes[c].at[pl.ds(p * blocks, blocks)]
+
+    def going_right(k, c):
+        p = jnp.maximum(part - k + 1, 0)
+        return send(
+            piece(p, c), piece(p, c), right_send.at[k, c], right_recv.at[k, c], "head", right
+        )
+
+    def going_left(k, c):
+        p = jnp.minimum(part + k - 1, head_size - 1)
+        return send(
+            piece(p, c), piece(p, c), left_send.at[k, c], left_recv.at[k, c], "head", left
+        )
+
+    sends_right = lambda k: jnp.logical_and(part - k + 1 >= 0, part < head_size - 1)
+    sends_left = lambda k: jnp.logical_and(part + k - 1 < head_size, part > 0)
+
+    def arrivals(k, c):
+        @pl.when(part - k >= 0)
+        def _():
+            going_right(k, c).wait_recv()
+
+        @pl.when(part + k < head_size)
+        def _():
+            going_left(k, c).wait_recv()
+
+    events = [("head", step) for step in head_steps] + [("seq", step) for step in seq_steps]
+
+    def root_copy(e):
+        axis, step = events[e]
+        at, length = (part, head_size) if axis == "head" else (shard, seq_size)
+        other = jnp.minimum(at + step, length - 1)
+        copy = send(root, root, root_send.at[e], root_recv.at[e], axis, other)
+        takes_part = shard == 0 if axis == "head" else shard >= 0
+        gives = jnp.logical_and(takes_part, jnp.logical_and(at < step, at + step < length))
+        gets = jnp.logical_and(takes_part, jnp.logical_and(at >= step, at < 2 * step))
+        return copy, gives, gets
+
+    def root_event(e):
+        if 0 < e <= len(events):
+            copy, _, gets = root_copy(e - 1)
+            pl.when(gets)(copy.wait_recv)
+        if e < len(events):
+            copy, gives, _ = root_copy(e)
+            pl.when(gives)(copy.start)
+
+    done = 0
+    for k in range(1, head_size):
+        for c in range(PIECES):
+            if k > 1:
+                arrivals(k - 1, c)
+            pl.when(sends_right(k))(going_right(k, c).start)
+            pl.when(sends_left(k))(going_left(k, c).start)
+            if c % 2 == 1:
+                root_event(done)
+                done += 1
+
+    def near_copy(c):
+        return send(
+            stage_near.at[c], in_near.at[c], near_send.at[c], near_recv.at[c],
+            "seq", jnp.minimum(shard + 1, seq_size - 1),
+        )
+
+    def far_copy(c):
+        return send(
+            stage_far.at[c], in_far.at[c], far_send.at[c], far_recv.at[c],
+            "seq", jnp.minimum(shard + 2, seq_size - 1),
+        )
+
+    def block_at(n):
+        return jnp.clip(wanted[n], 0, count - 1)
+
+    for c in range(PIECES):
+        arrivals(head_size - 1, c)
+        for n in range(blocks):
+            stage_far[c, n] = wholes[c][block_at(2 * blocks + n)]
+        pl.when(shard + 2 < seq_size)(far_copy(c).start)
+        for n in range(blocks):
+            stage_near[c, n] = wholes[c][block_at(blocks + n)]
+        pl.when(shard + 1 < seq_size)(near_copy(c).start)
+        root_event(done)
+        done += 1
+    while done <= len(events):
+        root_event(done)
+        done += 1
+    root_out[0] = root[...]
+    for c in range(PIECES):
+        kv, columns = piece_of(c, width)
+        for n in range(blocks):
+            rand[n, kv, :, columns] = wholes[c][block_at(n)]
+
+        @pl.when(shard >= 1)
+        def _(c=c, kv=kv, columns=columns):
+            near_copy(c).wait_recv()
+            for n in range(blocks):
+                rand[n, kv, :, columns] = jnp.where(
+                    back[n] == 1, in_near[c, n], rand[n, kv, :, columns]
+                )
+
+        @pl.when(shard >= 2)
+        def _(c=c, kv=kv, columns=columns):
+            far_copy(c).wait_recv()
+            for n in range(blocks):
+                rand[n, kv, :, columns] = jnp.where(
+                    back[n] == 2, in_far[c, n], rand[n, kv, :, columns]
+                )
+
+    for c in range(PIECES):
+        for k in range(1, head_size):
+            pl.when(sends_right(k))(going_right(k, c).wait_send)
+            pl.when(sends_left(k))(going_left(k, c).wait_send)
+        pl.when(shard + 2 < seq_size)(far_copy(c).wait_send)
+        pl.when(shard + 1 < seq_size)(near_copy(c).wait_send)
+    for e in range(len(events)):
+        copy, gives, _ = root_copy(e)
+        pl.when(gives)(copy.wait_send)
+
+
+def gather(wanted, back, own, head_size, seq_size):
+    blocks, _, _, width = own.shape
+    events = len(tree_steps(head_size)) + len(tree_steps(seq_size))
+    half = width * 2 // PIECES
+    vmem, smem = pltpu.MemorySpace.VMEM, pltpu.MemorySpace.SMEM
+    moved = pltpu.VMEM((PIECES, blocks, BLOCK, half), jnp.bfloat16)
+    line = pltpu.SemaphoreType.DMA((head_size, PIECES))
+    hop = pltpu.SemaphoreType.DMA((PIECES,))
+    return pl.pallas_call(
+        functools.partial(gather_kernel, head_size, seq_size),
+        in_specs=[
+            pl.BlockSpec(memory_space=smem),
+            pl.BlockSpec(memory_space=smem),
+            pl.BlockSpec(memory_space=vmem),
+        ],
+        out_specs=[pl.BlockSpec(memory_space=vmem)] * 2,
+        out_shape=[
+            jax.ShapeDtypeStruct(own.shape, jnp.bfloat16),
+            jax.ShapeDtypeStruct((1,) + own.shape[1:], jnp.bfloat16),
+        ],
+        scratch_shapes=[
+            *[pltpu.VMEM((blocks * head_size, BLOCK, half), jnp.bfloat16)] * PIECES,
+            pltpu.VMEM(own.shape[1:], jnp.bfloat16),
+            moved, moved, moved, moved,
+            line, line, line, line, hop, hop, hop, hop,
+            pltpu.SemaphoreType.DMA((events,)),
+            pltpu.SemaphoreType.DMA((events,)),
+        ],
+        compiler_params=pltpu.CompilerParams(
+            collective_id=0, has_side_effects=True, vmem_limit_bytes=40 * 1024 * 1024
+        ),
+        name="gather",
+    )(wanted, back, own)
+
+
+def scatter_kernel(
+    head_size, seq_size, *refs
+):
+    (placed, root_in, out, root_out, root, root_box, right_out, right_in, left_out, left_in,
+     right_send, right_recv, left_send, left_recv, root_send, root_recv) = refs
+    shard, part = lax.axis_index("seq"), lax.axis_index("head")
+    blocks, _, _, width = out.shape
+    head_steps, seq_steps = tree_steps(head_size), tree_steps(seq_size)
+    greet(head_steps, seq_steps, head_size, seq_size)
+    right = jnp.minimum(part + 1, head_size - 1)
+    left = jnp.maximum(part - 1, 0)
+    root[...] = root_in[...]
+
+    def piece(p, c):
+        kv, columns = piece_of(c, width)
+        return placed.at[pl.ds(p * blocks, blocks), kv, :, columns]
+
+    def going_right(d, c, source):
+        return send(
+            source, right_in.at[d, c], right_send.at[d, c], right_recv.at[d, c], "head", right
+        )
+
+    def going_left(d, c, source):
+        return send(
+            source, left_in.at[d, c], left_send.at[d, c], left_recv.at[d, c], "head", left
+        )
+
+    events = [("seq", step) for step in seq_steps[::-1]] + [
+        ("head", step) for step in head_steps[::-1]
+    ]
+
+    def root_copy(e):
+        axis, step = events[e]
+        at, length = (part, head_size) if axis == "head" else (shard, seq_size)
+        other = jnp.maximum(at - step, 0)
+        copy = send(root, root_box.at[e], root_send.at[e], root_recv.at[e], axis, other)
+        takes_part = shard == 0 if axis == "head" else shard >= 0
+        gives = jnp.logical_and(takes_part, jnp.logical_and(at >= step, at < 2 * step))
+        gets = jnp.logical_and(takes_part, jnp.logical_and(at < step, at + step < length))
+        return copy, gives, gets
+
+    def root_event(e):
+        if 0 < e <= len(events):
+            copy, _, gets = root_copy(e - 1)
+
+            @pl.when(gets)
+            def _():
+                copy.wait_recv()
+                root[...] += root_box[e - 1]
+
+        if e < len(events):
+            copy, gives, _ = root_copy(e)
+            pl.when(gives)(copy.start)
+
+    done = 0
+    for k in range(1, head_size):
+        to_right, to_left = head_size - k, k - 1
+        for c in range(PIECES):
+
+            @pl.when(part == 0)
+            def _(d=to_right, c=c):
+                going_right(d, c, piece(d, c)).start()
+
+            @pl.when(jnp.logical_and(part > 0, part < to_right))
+            def _(d=to_right, c=c):
+                going_right(d, c, right_out.at[d, c]).wait_recv()
+                right_out[d, c] = (
+                    piece(d, c)[...].astype(jnp.float32) + right_in[d, c].astype(jnp.float32)
+                ).astype(jnp.bfloat16)
+                going_right(d, c, right_out.at[d, c]).start()
+
+            @pl.when(part == head_size - 1)
+            def _(d=to_left, c=c):
+                going_left(d, c, piece(d, c)).start()
+
+            @pl.when(jnp.logical_and(part < head_size - 1, part > to_left))
+            def _(d=to_left, c=c):
+                going_left(d, c, left_out.at[d, c]).wait_recv()
+                left_out[d, c] = (
+                    piece(d, c)[...].astype(jnp.float32) + left_in[d, c].astype(jnp.float32)
+                ).astype(jnp.bfloat16)
+                going_left(d, c, left_out.at[d, c]).start()
+
+            if c % 2 == 1:
+                root_event(done)
+                done += 1
+    while done <= len(events):
+        root_event(done)
+        done += 1
+    for c in range(PIECES):
+        kv, columns = piece_of(c, width)
+        out[:, kv, :, columns] = piece(part, c)[...].astype(jnp.float32)
+
+        @pl.when(part > 0)
+        def _(c=c, kv=kv, columns=columns):
+            going_right(part, c, right_out.at[part, c]).wait_recv()
+            out[:, kv, :, columns] += right_in[part, c].astype(jnp.float32)
+
+        @pl.when(part < head_size - 1)
+        def _(c=c, kv=kv, columns=columns):
+            going_left(part, c, left_out.at[part, c]).wait_recv()
+            out[:, kv, :, columns] += left_in[part, c].astype(jnp.float32)
+
+    root_out[...] = root[...]
+    for d in range(head_size):
+        for c in range(PIECES):
+            pl.when(part < d)(going_right(d, c, right_out.at[d, c]).wait_send)
+            pl.when(part > d)(going_left(d, c, left_out.at[d, c]).wait_send)
+    for e in range(len(events)):
+        copy, gives, _ = root_copy(e)
+        pl.when(gives)(copy.wait_send)
+
+
+def scatter(placed, root, head_size, seq_size):
+    count, _, _, width = placed.shape
+    blocks = count // head_size
+    events = len(tree_steps(head_size)) + len(tree_steps(seq_size))
+    half = width * 2 // PIECES
+    vmem = pltpu.MemorySpace.VMEM
+    box = pltpu.VMEM((head_size, PIECES, blocks, BLOCK, half), jnp.bfloat16)
+    line = pltpu.SemaphoreType.DMA((head_size, PIECES))
+    return pl.pallas_call(
+        functools.partial(scatter_kernel, head_size, seq_size),
+        in_specs=[pl.BlockSpec(memory_space=vmem)] * 2,
+        out_specs=[pl.BlockSpec(memory_space=vmem)] * 2,
+        out_shape=[
+            jax.ShapeDtypeStruct((blocks,) + placed.shape[1:], jnp.float32),
+            jax.ShapeDtypeStruct(root.shape, jnp.float32),
+        ],
+        scratch_shapes=[
+            pltpu.VMEM(root.shape, jnp.float32),
+            pltpu.VMEM((events,) + root.shape, jnp.float32),
+            box, box, box, box,
+            line, line, line, line,
+            pltpu.SemaphoreType.DMA((events,)),
+            pltpu.SemaphoreType.DMA((events,)),
+        ],
+        compiler_params=pltpu.CompilerParams(
+            collective_id=1, has_side_effects=True, vmem_limit_bytes=48 * 1024 * 1024
+        ),
+        name="scatter",
+    )(placed, root)
+
+
 def local(queries, key_rows, value_rows, upstream, ancestors):
     tokens, width = key_rows.shape
     blocks = tokens // BLOCK
@@ -250,51 +592,38 @@
         [key_rows.reshape(blocks, BLOCK, width), value_rows.reshape(blocks, BLOCK, width)], 1
     )
     chunk_heads = width // HEAD_SIZE // CHUNKS
-    chunk_width = chunk_heads * HEAD_SIZE
+    head_size, seq_size = lax.axis_size("head"), length
     is_first = (shard == 0) & (part == 0)
     edge = shifted(own[-1:], both, 1)
-    root = jnp.where(is_first, own[:1], jnp.zeros_like(own[:1]))
-    root = spread_from_first(spread_from_first(root, "head"), "seq")
-
-    def at(x, index):
-        return jnp.take(x, jnp.clip(index, 0, shard_blocks - 1), axis=0)
-
-    rands = []
-    back = shard - last_entry // shard_blocks
-    for c in range(CHUNKS):
-        piece = own[..., c * chunk_width : (c + 1) * chunk_width]
-        whole = lax.all_gather(piece, "head", axis=0, tiled=True)
-        near = shifted(at(whole, wanted_near), "seq", 1)
-        far = shifted(at(whole, wanted_far), "seq", 2)
-        pick = back[:, None, None, None]
-        rands.append(
-            jnp.where(pick == 0, at(whole, wanted_own), jnp.where(pick == 1, near, far))
-        )
+    back = (shard - last_entry // shard_blocks).astype(jnp.int32)
+    rand, root = gather(wanted, back, own, head_size, seq_size)
     outs = None
-    key_grads, value_grads = [], []
+    g_owns, g_prevs, placed, g_roots = [], [], [], []
     for c in range(CHUNKS):
         attended, query_grad, g_own, g_prev, g_rand, g_root = attention(
-            info, queries, upstream, own, edge, root, rands[c], outs, c, chunk_heads
+            info, queries, upstream, own, edge, root, rand, outs, c, chunk_heads
         )
         outs = (attended, query_grad)
         near = shifted(g_rand, "seq", -1)
         far = shifted(g_rand, "seq", -2)
-        placed = place(wanted, g_rand, near, far, shard_blocks)
-        summed = lax.psum_scatter(placed, "head", scatter_dimension=0, tiled=True)
-        g_root = sum_to_first(sum_to_first(g_root, "seq"), "head")
-        g_edge = shifted(g_prev[:1].astype(jnp.bfloat16), both, -1).astype(jnp.float32)
-        total = g_own + summed.astype(jnp.float32)
-        total = total + jnp.concatenate([g_prev[1:], g_edge], 0)
-        head_of_row = jnp.where(is_first, g_root, 0.0)
-        total = jnp.concatenate([total[:1] + head_of_row[None], total[1:]], 0)
-        total = total.astype(jnp.bfloat16)
-        key_grads.append(total[:, 0].reshape(tokens, chunk_width))
-        value_grads.append(total[:, 1].reshape(tokens, chunk_width))
+        placed.append(place(wanted, g_rand, near, far, shard_blocks))
+        g_owns.append(g_own)
+        g_prevs.append(g_prev)
+        g_roots.append(g_root)
+    g_own, g_prev = jnp.concatenate(g_owns, -1), jnp.concatenate(g_prevs, -1)
+    g_edge = shifted(g_prev[:1].astype(jnp.bfloat16), both, -1).astype(jnp.float32)
+    summed, g_root = scatter(
+        jnp.concatenate(placed, -1), jnp.concatenate(g_roots, -1), head_size, seq_size
+    )
+    total = g_own + summed + jnp.concatenate([g_prev[1:], g_edge], 0)
+    head_of_row = jnp.where(is_first, g_root, 0.0)
+    total = jnp.concatenate([total[:1] + head_of_row[None], total[1:]], 0)
+    total = total.astype(jnp.bfloat16)
     return (
         outs[0],
         outs[1],
-        jnp.concatenate(key_grads, 1),
-        jnp.concatenate(value_grads, 1),
+        total[:, 0].reshape(tokens, width),
+        total[:, 1].reshape(tokens, width),
     )
 
 

time: 375 us -> 303 us (0.81)
  Pallas kernels: 46 us -> 242 us
  waiting for transfers between devices: 214 us -> 25.1 us
  starting transfers between devices: 50.9 us -> 14.1 us
  local copies, waits for them, and re-layouts: 32.4 us -> 10.4 us
  between operations: 14.5 us -> 0.91 us
  other arithmetic: 16.5 us -> 10.2 us
    pallas_call x0 -> x2, Pallas kernels: none -> 196 us  [the longest x1 112 us: scatter(): pl.pallas_call(functools.partial(scatter_kernel, head_size, seq_size), in...]
    ppermute x15 -> x0, waiting for transfers between devices: 103 us -> none  [the longest x10 54.9 us: sum_to_first(): x = x + lax.ppermute(x, axis, pairs)]
    all_gather x2 -> x0, waiting for transfers between devices: 66.2 us -> none  [local(): whole = lax.all_gather(piece, 'head', axis=0, tiled=True)]
    ppermute x15 -> x0, starting transfers between devices: 25.6 us -> none  [the longest x10 13 us: sum_to_first(): x = x + lax.ppermute(x, axis, pairs)]
    ppermute x13 -> x8, waiting for transfers between devices: 43.9 us -> 25.1 us  [shifted(): return lax.ppermute(x, axis, pairs)]
    gather x6 -> x0, local copies, waits for them, and re-layouts: 13 us -> none  [at(): return jnp.take(x, jnp.clip(index, 0, shard_blocks - 1), axis=0)]
    ppermute x13 -> x8, starting transfers between devices: 25.2 us -> 14.1 us  [shifted(): return lax.ppermute(x, axis, pairs)]
    unnamed x54 -> x21, local copies, waits for them, and re-layouts: 17.9 us -> 7.15 us
  transfers between devices with their start and end apart: 32 -> 8, of which waited for: 19 -> 3; matrix products, arithmetic and copies ran while one was open for 7% -> 2% of each run, Pallas kernels for 6% -> 29%
where the time goes in v2:
time: 303 us; the launch traced here: 302 us
  Pallas kernels  242 us (80%)
  waiting for transfers between devices  25.1 us (8%)
  starting transfers between devices  14.1 us (5%)
  local copies, waits for them, and re-layouts  10.4 us (3%)
  other arithmetic  10.2 us (3%)
    pallas_call x1, Pallas kernels, scatter(): pl.pallas_call(functools.partial(scatter_kernel, head_size, seq_size), in...  112 us
    pallas_call x1, Pallas kernels, gather(): pl.pallas_call(functools.partial(gather_kernel, head_size, seq_size), in_...  84 us
    pallas_call x2, Pallas kernels, attention(): pl.pallas_call(functools.partial(attention_kernel, groups=groups, aliased...  36 us
    ppermute x8, waiting for transfers between devices, shifted(): return lax.ppermute(x, axis, pairs)  25.1 us
    ppermute x8, starting transfers between devices, shifted(): return lax.ppermute(x, axis, pairs)  14.1 us
    pallas_call x2, Pallas kernels, place(): pl.pallas_call(place_kernel, grid_spec=pltpu.PrefetchScalarGridSpec(num_s...  9.95 us
    unnamed x21, local copies, waits for them, and re-layouts  7.15 us
  transfers between devices with their start and end apart: 8, of which 3 were waited for; matrix products, arithmetic and copies ran while one was open for 2% of the time, Pallas kernels for 29%

profile of v2, /device:TPU:0, one launch (start us, length us, event | category | flops | bytes accessed | tf_op | source)
XLA Modules:
  0.0 302.5 jit_solution(2129799574755573258)
XLA Ops:
  0.7 0.7 copy-done
  1.4 1.3 collective-permute-start.1
  2.7 1.3 collective-permute-start.2
  4.0 1.0 fusion.3
  5.0 4.9 %collective-permute-start = (bf16[1,2,64,1024]{3,2,1,0:T(8,128)(2,1)S(1)}, bf16[1,2,64,1024]{3,2,1,0:T(8,128)(2,1)S(1)}, u32[]{:S(2)}, u32[]{:S(2)}) collective-permute-start(bf16[1,2,64,1024]{3,2,1,0:T(8,128)(2,1)S(1)} %fusion.3), channel_id=1, source_target_pairs={{0,1},{1,2},{2,3},{3,4},{4,5},{5,6},{6,7},{7,8},{8,9},{9,10},{10,1... | collective-permute-start | bytes 786440 | tf_op jit(solution)/shard_map/ppermute | solution.py:20
  10.0 1.3 pad_maximum_fusion.1.own.own_ref.before_ref
  11.3 0.1 copy.12
  11.7 84.0 %gather.1 = (bf16[4,2,64,1024]{3,2,1,0:T(8,128)(2,1)S(1)}, bf16[1,2,64,1024]{3,2,1,0:T(8,128)(2,1)S(1)}) custom-call(s32[12]{0:T(128)S(1)} %pad_add_fusion.1.wanted.index, s32[4]{0:T(128)S(1)} %get-tuple-element.38.back, bf16[4,2,64,1024]{3,2,1,0:T(8,128)(2,1)S(1)} %pad_maximum_fusion.1.own.own_ref.before_ref), custom_call_target="tpu_custom_call" | custom-call | tf_op jit(solution)/shard_map/gather/pallas_call | solution.py:395
  95.7 2.2 copy-done.1
  97.8 2.2 copy-done.2
  100.0 17.9 %attention.2 = (bf16[256,8192]{1,0:T(8,128)(2,1)}, bf16[256,8192]{1,0:T(8,128)(2,1)}, f32[4,2,64,512]{3,2,1,0:T(8,128)S(1)}, f32[4,2,64,512]{3,2,1,0:T(8,128)S(1...) custom-call(s32[9]{0:T(128)S(1)} %pad_add_fusion.info, bf16[256,8192]{1,0:T(8,128)(2,1)S(1)} %copy-done.1, ...), custom_call_target="tpu_custom_call" | custom-call | flops 3221225472 | bytes 8388608 | tf_op jit(solution)/shard_map/attention/pallas_call | solution.py:129
  117.9 0.7 copy-done.3
  118.6 18.1 %attention.3 = (bf16[256,8192]{1,0:T(8,128)(2,1)}, bf16[256,8192]{1,0:T(8,128)(2,1)}, f32[4,2,64,512]{3,2,1,0:T(8,128)S(1)}, f32[4,2,64,512]{3,2,1,0:T(8,128)S(1...) custom-call(s32[9]{0:T(128)S(1)} %pad_add_fusion.info, ...), custom_call_target="tpu_custom_call", output_to_operand_aliasing={{0}: (8, {}), {1}: (9, {})} | custom-call | flops 3221225472 | bytes 8388608 | tf_op jit(solution)/shard_map/attention/pallas_call | solution.py:129
  136.8 1.3 collective-permute-start.6
  138.1 1.3 collective-permute-start.5
  139.4 1.3 collective-permute-start.4
  140.7 1.3 collective-permute-start.3
  142.0 0.1 constant_dynamic-update-slice_fusion
  142.2 1.3 copy-done.9
  143.5 1.4 collective-permute-start.7
  144.9 2.8 slice.40
  147.8 4.2 %collective-permute-done.7 = bf16[1,2,64,1024]{3,2,1,0:T(8,128)(2,1)} collective-permute-done((bf16[1,2,64,1024]{3,2,1,0:T(8,128)(2,1)S(1)}, bf16[1,2,64,1024]{3,2,1,0:T(8,128)(2,1)}, u32[]{:S(2)}, u32[]{:S(2)}) %collective-permute-start.7) | collective-permute-done | bytes 262176 | tf_op jit(solution)/shard_map/ppermute | solution.py:20
  152.0 1.0 convert_element_type.13
  153.0 7.5 %collective-permute-done.6.far_ref = bf16[4,2,64,512]{3,2,1,0:T(8,128)(2,1)} collective-permute-done((bf16[4,2,64,512]{3,2,1,0:T(8,128)(2,1)}, bf16[4,2,64,512]{3,2,1,0:T(8,128)(2,1)}, u32[]{:S(2)}, u32[]{:S(2)}) %collective-permute-start.6) | collective-permute-done | bytes 524320 | tf_op jit(solution)/shard_map/ppermute | solution.py:20
  160.5 4.9 %place.3 = bf16[16,2,64,512]{3,2,1,0:T(8,128)(2,1)} custom-call(s32[12]{0:T(128)} %copy-done.7, bf16[4,2,64,512]{3,2,1,0:T(8,128)(2,1)} %get-tuple-element.29.own_ref, bf16[4,2,64,512]{3,2,1,0:T(8,128)(2,1)} %collective-permute-done.5.near_ref, bf16[4,2,64,512]{3,2,1,0:T(8,128)(2,1)} %collective-permute-done.6.far_ref), custom_call_target="tpu_custom_call" | custom-call | flops 1048576 | bytes 3670016 | tf_op jit(solution)/shard_map/place/pallas_call | solution.py:183
  165.4 13.3 %collective-permute-done.4.far_ref = bf16[4,2,64,512]{3,2,1,0:T(8,128)(2,1)} collective-permute-done((bf16[4,2,64,512]{3,2,1,0:T(8,128)(2,1)}, bf16[4,2,64,512]{3,2,1,0:T(8,128)(2,1)}, u32[]{:S(2)}, u32[]{:S(2)}) %collective-permute-start.4) | collective-permute-done | bytes 524320 | tf_op jit(solution)/shard_map/ppermute | solution.py:20
  178.8 5.0 %place.2 = bf16[16,2,64,512]{3,2,1,0:T(8,128)(2,1)} custom-call(s32[12]{0:T(128)} %copy-done.7, bf16[4,2,64,512]{3,2,1,0:T(8,128)(2,1)} %get-tuple-element.28.own_ref, bf16[4,2,64,512]{3,2,1,0:T(8,128)(2,1)} %collective-permute-done.3.near_ref, bf16[4,2,64,512]{3,2,1,0:T(8,128)(2,1)} %collective-permute-done.4.far_ref), custom_call_target="tpu_custom_call" | custom-call | flops 1048576 | bytes 3670016 | tf_op jit(solution)/shard_map/place/pallas_call | solution.py:183
  183.8 4.8 %pad_maximum_fusion.refs_0_ = bf16[16,2,64,1024]{3,2,1,0:T(8,128)(2,1)} fusion(bf16[16,2,64,512]{3,2,1,0:T(8,128)(2,1)} %place.3, bf16[16,2,64,512]{3,2,1,0:T(8,128)(2,1)} %place.2), kind=kLoop, calls=%fused_computation | loop fusion | flops 8388608 | bytes 8388608 | tf_op jit(solution)/shard_map/concatenate | solution.py:616
  188.6 111.9 %scatter.1 = (f32[4,2,64,1024]{3,2,1,0:T(8,128)S(1)}, f32[2,64,1024]{2,1,0:T(8,128)S(1)}) custom-call(bf16[16,2,64,1024]{3,2,1,0:T(8,128)(2,1)} %pad_maximum_fusion.refs_0_, f32[2,64,1024]{2,1,0:T(8,128)S(1)} %pad_maximum_fusion.3.refs_1_), custom_call_target="tpu_custom_call" | custom-call | tf_op jit(solution)/shard_map/scatter/pallas_call | solution.py:543
  300.5 0.7 fusion
  301.2 0.1 slice.71
  301.4 1.1 pad_maximum_fusion.2
  (34 shorter events, 0.6 us)
Async XLA Ops:
  0.6 0.7 copy-start
  1.4 10.2 %collective-permute-start.1 = (s32[4]{0:T(128)S(1)}, s32[4]{0:T(128)S(1)}, u32[]{:S(2)}, u32[]{:S(2)}) collective-permute-start(s32[4]{0:T(128)S(1)} %slice_bitcast_fusion), channel_id=1, source_target_pairs={{4,0},{8,4},{12,8},{16,12},{20,16},{24,20},{28,24},{5,1},{9,5},{13... | collective-permute-start | bytes 56 | tf_op jit(solution)/shard_map/ppermute | solution.py:20
  2.7 8.9 %collective-permute-start.2 = (s32[4]{0:T(128)S(1)}, s32[4]{0:T(128)S(1)}, u32[]{:S(2)}, u32[]{:S(2)}) collective-permute-start(s32[4]{0:T(128)S(1)} %slice_bitcast_fusion), channel_id=1, source_target_pairs={{8,0},{12,4},{16,8},{20,12},{24,16},{28,20},{9,1},{13,5},{17,9},{2... | collective-permute-start | bytes 56 | tf_op jit(solution)/shard_map/ppermute | solution.py:20
  5.0 90.7 %collective-permute-start = (bf16[1,2,64,1024]{3,2,1,0:T(8,128)(2,1)S(1)}, bf16[1,2,64,1024]{3,2,1,0:T(8,128)(2,1)S(1)}, u32[]{:S(2)}, u32[]{:S(2)}) collective-permute-start(bf16[1,2,64,1024]{3,2,1,0:T(8,128)(2,1)S(1)} %fusion.3), channel_id=1, source_target_pairs={{0,1},{1,2},{2,3},{3,4},{4,5},{5,6},{6,7},{7,8},{8,9},{9,10},{10,1... | collective-permute-start | bytes 786440 | tf_op jit(solution)/shard_map/ppermute | solution.py:20
  11.7 106.2 %copy-start.7 = (s32[12]{0:T(128)}, s32[12]{0:T(128)S(1)}, u32[]{:S(2)}) copy-start(s32[12]{0:T(128)S(1)} %pad_add_fusion.1.wanted.index) | copy-start | bytes 148
  95.6 2.2 copy-start.1
  97.8 2.2 copy-start.2
  117.9 0.7 copy-start.3
  136.8 5.4 %copy-start.5 = (f32[2,64,512]{2,1,0:T(8,128)}, f32[2,64,512]{2,1,0:T(8,128)S(1)}, u32[]{:S(2)}) copy-start(f32[2,64,512]{2,1,0:T(8,128)S(1)} %get-tuple-element.31) | copy-start | bytes 786436
  136.8 23.7 %collective-permute-start.6 = (bf16[4,2,64,512]{3,2,1,0:T(8,128)(2,1)}, bf16[4,2,64,512]{3,2,1,0:T(8,128)(2,1)}, u32[]{:S(2)}, u32[]{:S(2)}) collective-permute-start(bf16[4,2,64,512]{3,2,1,0:T(8,128)(2,1)} %get-tuple-element.29.own_ref), channel_id=1, source_target_pairs={{8,0},{12,4},{16,8},{20,12},{24,16},{28,20},{9,1},{13,5},{17,9},{2... | collective-permute-start | bytes 1572872 | tf_op jit(solution)/shard_map/ppermute | solution.py:20
  138.1 22.4 %collective-permute-start.5 = (bf16[4,2,64,512]{3,2,1,0:T(8,128)(2,1)}, bf16[4,2,64,512]{3,2,1,0:T(8,128)(2,1)}, u32[]{:S(2)}, u32[]{:S(2)}) collective-permute-start(bf16[4,2,64,512]{3,2,1,0:T(8,128)(2,1)} %get-tuple-element.29.own_ref), channel_id=1, source_target_pairs={{4,0},{8,4},{12,8},{16,12},{20,16},{24,20},{28,24},{5,1},{9,5},{13... | collective-permute-start | bytes 1572872 | tf_op jit(solution)/shard_map/ppermute | solution.py:20
  139.4 39.4 %collective-permute-start.4 = (bf16[4,2,64,512]{3,2,1,0:T(8,128)(2,1)}, bf16[4,2,64,512]{3,2,1,0:T(8,128)(2,1)}, u32[]{:S(2)}, u32[]{:S(2)}) collective-permute-start(bf16[4,2,64,512]{3,2,1,0:T(8,128)(2,1)} %get-tuple-element.28.own_ref), channel_id=1, source_target_pairs={{8,0},{12,4},{16,8},{20,12},{24,16},{28,20},{9,1},{13,5},{17,9},{2... | collective-permute-start | bytes 1572872 | tf_op jit(solution)/shard_map/ppermute | solution.py:20
  140.7 38.1 %collective-permute-start.3 = (bf16[4,2,64,512]{3,2,1,0:T(8,128)(2,1)}, bf16[4,2,64,512]{3,2,1,0:T(8,128)(2,1)}, u32[]{:S(2)}, u32[]{:S(2)}) collective-permute-start(bf16[4,2,64,512]{3,2,1,0:T(8,128)(2,1)} %get-tuple-element.28.own_ref), channel_id=1, source_target_pairs={{4,0},{8,4},{12,8},{16,12},{20,16},{24,20},{28,24},{5,1},{9,5},{13... | collective-permute-start | bytes 1572872 | tf_op jit(solution)/shard_map/ppermute | solution.py:20
  142.2 1.3 copy-start.9
  142.2 5.5 %copy-start.4 = (f32[2,64,512]{2,1,0:T(8,128)S(1)}, f32[2,64,512]{2,1,0:T(8,128)}, u32[]{:S(2)}) copy-start(f32[2,64,512]{2,1,0:T(8,128)} %copy-done.3) | copy-start | bytes 786436
  143.5 4.2 %copy-start.6 = (f32[2,64,512]{2,1,0:T(8,128)S(1)}, f32[2,64,512]{2,1,0:T(8,128)}, u32[]{:S(2)}) copy-start(f32[2,64,512]{2,1,0:T(8,128)} %copy-done.5) | copy-start | bytes 786436
  143.5 8.5 %collective-permute-start.7 = (bf16[1,2,64,1024]{3,2,1,0:T(8,128)(2,1)S(1)}, bf16[1,2,64,1024]{3,2,1,0:T(8,128)(2,1)}, u32[]{:S(2)}, u32[]{:S(2)}) collective-permute-start(bf16[1,2,64,1024]{3,2,1,0:T(8,128)(2,1)S(1)} %slice.72), channel_id=1, source_target_pairs={{1,0},{2,1},{3,2},{4,3},{5,4},{6,5},{7,6},{8,7},{9,8},{10,9},{11,1... | collective-permute-start | bytes 786440 | tf_op jit(solution)/shard_map/ppermute | solution.py:20
  188.6 111.9 %copy-start.8 = (f32[3,2,64,1024]{3,2,1,0:T(8,128)S(1)}, f32[3,2,64,1024]{3,2,1,0:T(8,128)}, u32[]{:S(2)}) copy-start(f32[3,2,64,1024]{3,2,1,0:T(8,128)} %slice.40) | copy-start | bytes 4718596

commit v3 on v2

--- a/solution.py
+++ b/solution.py
@@ -151,7 +151,7 @@
         ],
         input_output_aliases=aliases,
         cost_estimate=pl.CostEstimate(
-            flops=12 * elements * HEAD_SIZE,
+            flops=80 * elements * HEAD_SIZE,
             transcendentals=elements,
             bytes_accessed=blocks * chunk_heads * wide * BLOCK * 8,
         ),
@@ -199,7 +199,7 @@
     )(index, own, near, far)
 
 
-PIECES = 4
+PIECES = 2 * CHUNKS
 
 
 def tree_steps(length):
@@ -422,7 +422,8 @@
 def scatter_kernel(
     head_size, seq_size, *refs
 ):
-    (placed, root_in, out, root_out, root, root_box, right_out, right_in, left_out, left_in,
+    placed, refs = refs[:CHUNKS], refs[CHUNKS:]
+    (root_in, out, root_out, root, root_box, right_out, right_in, left_out, left_in,
      right_send, right_recv, left_send, left_recv, root_send, root_recv) = refs
     shard, part = lax.axis_index("seq"), lax.axis_index("head")
     blocks, _, _, width = out.shape
@@ -433,8 +434,7 @@
     root[...] = root_in[...]
 
     def piece(p, c):
-        kv, columns = piece_of(c, width)
-        return placed.at[pl.ds(p * blocks, blocks), kv, :, columns]
+        return placed[c % CHUNKS].at[pl.ds(p * blocks, blocks), c // CHUNKS]
 
     def going_right(d, c, source):
         return send(
@@ -502,9 +502,8 @@
                 ).astype(jnp.bfloat16)
                 going_left(d, c, left_out.at[d, c]).start()
 
-            if c % 2 == 1:
-                root_event(done)
-                done += 1
+            root_event(done)
+            done += 1
     while done <= len(events):
         root_event(done)
         done += 1
@@ -533,7 +532,8 @@
 
 
 def scatter(placed, root, head_size, seq_size):
-    count, _, _, width = placed.shape
+    count = placed[0].shape[0]
+    width = root.shape[-1]
     blocks = count // head_size
     events = len(tree_steps(head_size)) + len(tree_steps(seq_size))
     half = width * 2 // PIECES
@@ -542,10 +542,10 @@
     line = pltpu.SemaphoreType.DMA((head_size, PIECES))
     return pl.pallas_call(
         functools.partial(scatter_kernel, head_size, seq_size),
-        in_specs=[pl.BlockSpec(memory_space=vmem)] * 2,
+        in_specs=[pl.BlockSpec(memory_space=vmem)] * (CHUNKS + 1),
         out_specs=[pl.BlockSpec(memory_space=vmem)] * 2,
         out_shape=[
-            jax.ShapeDtypeStruct((blocks,) + placed.shape[1:], jnp.float32),
+            jax.ShapeDtypeStruct((blocks, 2, BLOCK, width), jnp.float32),
             jax.ShapeDtypeStruct(root.shape, jnp.float32),
         ],
         scratch_shapes=[
@@ -560,7 +560,7 @@
             collective_id=1, has_side_effects=True, vmem_limit_bytes=48 * 1024 * 1024
         ),
         name="scatter",
-    )(placed, root)
+    )(*placed, root)
 
 
 def local(queries, key_rows, value_rows, upstream, ancestors):
@@ -613,7 +613,7 @@
     g_own, g_prev = jnp.concatenate(g_owns, -1), jnp.concatenate(g_prevs, -1)
     g_edge = shifted(g_prev[:1].astype(jnp.bfloat16), both, -1).astype(jnp.float32)
     summed, g_root = scatter(
-        jnp.concatenate(placed, -1), jnp.concatenate(g_roots, -1), head_size, seq_size
+        placed, jnp.concatenate(g_roots, -1), head_size, seq_size
     )
     total = g_own + summed + jnp.concatenate([g_prev[1:], g_edge], 0)
     head_of_row = jnp.where(is_first, g_root, 0.0)

time: 303 us -> 302 us (level)
  other arithmetic: 10.2 us -> 5.37 us
    concatenate x1 -> x0, other arithmetic: 4.82 us -> none  [local(): jnp.concatenate(placed, -1)]
    unnamed x21 -> x23, local copies, waits for them, and re-layouts: 7.15 us -> 9.06 us
where the time goes in v3:
time: 302 us; the launch traced here: 301 us
  Pallas kernels  244 us (81%)
  waiting for transfers between devices  25.1 us (8%)
  starting transfers between devices  14.1 us (5%)
  local copies, waits for them, and re-layouts  12.3 us (4%)
  other arithmetic  5.37 us (2%)
    pallas_call x1, Pallas kernels, scatter(): pl.pallas_call(functools.partial(scatter_kernel, head_size, seq_size), in...  114 us
    pallas_call x1, Pallas kernels, gather(): pl.pallas_call(functools.partial(gather_kernel, head_size, seq_size), in_...  84 us
    pallas_call x2, Pallas kernels, attention(): pl.pallas_call(functools.partial(attention_kernel, groups=groups, aliased...  36 us
    ppermute x8, waiting for transfers between devices, shifted(): return lax.ppermute(x, axis, pairs)  25.1 us
    ppermute x8, starting transfers between devices, shifted(): return lax.ppermute(x, axis, pairs)  14.1 us
    pallas_call x2, Pallas kernels, place(): pl.pallas_call(place_kernel, grid_spec=pltpu.PrefetchScalarGridSpec(num_s...  9.85 us
    unnamed x23, local copies, waits for them, and re-layouts  9.06 us
  transfers between devices with their start and end apart: 8, of which 3 were waited for; matrix products, arithmetic and copies ran while one was open for 2% of the time, Pallas kernels for 29%

profile of v3, /device:TPU:0, one launch (start us, length us, event | category | flops | bytes accessed | tf_op | source)
XLA Modules:
  0.0 301.3 jit_solution(511275025134213938)
XLA Ops:
  0.7 0.7 copy-done
  1.4 1.3 collective-permute-start.1
  2.7 1.3 collective-permute-start.2
  4.0 1.0 fusion.3
  5.0 4.9 %collective-permute-start = (bf16[1,2,64,1024]{3,2,1,0:T(8,128)(2,1)S(1)}, bf16[1,2,64,1024]{3,2,1,0:T(8,128)(2,1)S(1)}, u32[]{:S(2)}, u32[]{:S(2)}) collective-permute-start(bf16[1,2,64,1024]{3,2,1,0:T(8,128)(2,1)S(1)} %fusion.3), channel_id=1, source_target_pairs={{0,1},{1,2},{2,3},{3,4},{4,5},{5,6},{6,7},{7,8},{8,9},{9,10},{10,1... | collective-permute-start | bytes 786440 | tf_op jit(solution)/shard_map/ppermute | solution.py:20
  10.0 1.3 pad_maximum_fusion.own.own_ref.before_ref
  11.3 0.1 copy.12
  11.7 84.0 %gather.1 = (bf16[4,2,64,1024]{3,2,1,0:T(8,128)(2,1)S(1)}, bf16[1,2,64,1024]{3,2,1,0:T(8,128)(2,1)S(1)}) custom-call(s32[12]{0:T(128)S(1)} %pad_add_fusion.1.wanted.index, s32[4]{0:T(128)S(1)} %get-tuple-element.38.back, bf16[4,2,64,1024]{3,2,1,0:T(8,128)(2,1)S(1)} %pad_maximum_fusion.own.own_ref.before_ref), custom_call_target="tpu_custom_call" | custom-call | tf_op jit(solution)/shard_map/gather/pallas_call | solution.py:395
  95.7 2.3 copy-done.5
  97.9 2.2 copy-done.6
  100.1 17.9 %attention.2 = (bf16[256,8192]{1,0:T(8,128)(2,1)}, bf16[256,8192]{1,0:T(8,128)(2,1)}, f32[4,2,64,512]{3,2,1,0:T(8,128)S(1)}, f32[4,2,64,512]{3,2,1,0:T(8,128)S(1...) custom-call(s32[9]{0:T(128)S(1)} %pad_add_fusion.info, bf16[256,8192]{1,0:T(8,128)(2,1)S(1)} %copy-done.5, ...), custom_call_target="tpu_custom_call" | custom-call | flops 21474836480 | bytes 8388608 | tf_op jit(solution)/shard_map/attention/pallas_call | solution.py:129
  118.0 0.9 copy-done.8
  119.0 18.1 %attention.3 = (bf16[256,8192]{1,0:T(8,128)(2,1)}, bf16[256,8192]{1,0:T(8,128)(2,1)}, f32[4,2,64,512]{3,2,1,0:T(8,128)S(1)}, f32[4,2,64,512]{3,2,1,0:T(8,128)S(1...) custom-call(s32[9]{0:T(128)S(1)} %pad_add_fusion.info, ...), custom_call_target="tpu_custom_call", output_to_operand_aliasing={{0}: (8, {}), {1}: (9, {})} | custom-call | flops 21474836480 | bytes 8388608 | tf_op jit(solution)/shard_map/attention/pallas_call | solution.py:129
  137.1 1.3 collective-permute-start.6
  138.4 1.3 collective-permute-start.5
  139.7 1.3 collective-permute-start.4
  141.0 1.3 collective-permute-start.3
  142.4 0.1 constant_dynamic-update-slice_fusion
  142.5 1.3 copy-done.10
  143.8 1.4 collective-permute-start.7
  145.3 2.8 slice.40
  148.1 4.3 %collective-permute-done.7 = bf16[1,2,64,1024]{3,2,1,0:T(8,128)(2,1)} collective-permute-done((bf16[1,2,64,1024]{3,2,1,0:T(8,128)(2,1)S(1)}, bf16[1,2,64,1024]{3,2,1,0:T(8,128)(2,1)}, u32[]{:S(2)}, u32[]{:S(2)}) %collective-permute-start.7) | collective-permute-done | bytes 262176 | tf_op jit(solution)/shard_map/ppermute | solution.py:20
  152.3 1.0 convert_element_type.13
  153.3 7.5 %collective-permute-done.6.far_ref = bf16[4,2,64,512]{3,2,1,0:T(8,128)(2,1)} collective-permute-done((bf16[4,2,64,512]{3,2,1,0:T(8,128)(2,1)}, bf16[4,2,64,512]{3,2,1,0:T(8,128)(2,1)}, u32[]{:S(2)}, u32[]{:S(2)}) %collective-permute-start.6) | collective-permute-done | bytes 524320 | tf_op jit(solution)/shard_map/ppermute | solution.py:20
  160.8 4.9 %place.3.refs_1_ = bf16[16,2,64,512]{3,2,1,0:T(8,128)(2,1)} custom-call(s32[12]{0:T(128)} %copy-done.4, bf16[4,2,64,512]{3,2,1,0:T(8,128)(2,1)} %get-tuple-element.29.own_ref, bf16[4,2,64,512]{3,2,1,0:T(8,128)(2,1)} %collective-permute-done.5.near_ref, bf16[4,2,64,512]{3,2,1,0:T(8,128)(2,1)} %collective-permute-done.6.far_ref), custom_call_target="tpu_custom_call" | custom-call | flops 1048576 | bytes 3670016 | tf_op jit(solution)/shard_map/place/pallas_call | solution.py:183
  165.7 13.4 %collective-permute-done.4.far_ref = bf16[4,2,64,512]{3,2,1,0:T(8,128)(2,1)} collective-permute-done((bf16[4,2,64,512]{3,2,1,0:T(8,128)(2,1)}, bf16[4,2,64,512]{3,2,1,0:T(8,128)(2,1)}, u32[]{:S(2)}, u32[]{:S(2)}) %collective-permute-start.4) | collective-permute-done | bytes 524320 | tf_op jit(solution)/shard_map/ppermute | solution.py:20
  179.1 4.9 %place.2.refs_0_ = bf16[16,2,64,512]{3,2,1,0:T(8,128)(2,1)} custom-call(s32[12]{0:T(128)} %copy-done.4, bf16[4,2,64,512]{3,2,1,0:T(8,128)(2,1)} %get-tuple-element.28.own_ref, bf16[4,2,64,512]{3,2,1,0:T(8,128)(2,1)} %collective-permute-done.3.near_ref, bf16[4,2,64,512]{3,2,1,0:T(8,128)(2,1)} %collective-permute-done.4.far_ref), custom_call_target="tpu_custom_call" | custom-call | flops 1048576 | bytes 3670016 | tf_op jit(solution)/shard_map/place/pallas_call | solution.py:183
  184.0 1.6 copy-done.1
  185.6 113.7 %scatter.1 = (f32[4,2,64,1024]{3,2,1,0:T(8,128)S(1)}, f32[2,64,1024]{2,1,0:T(8,128)S(1)}) custom-call(bf16[16,2,64,512]{3,2,1,0:T(8,128)(2,1)S(1)} %copy-done.1, bf16[16,2,64,512]{3,2,1,0:T(8,128)(2,1)} %place.3.refs_1_, f32[2,64,1024]{2,1,0:T(8,128)S(1)} %pad_maximum_fusion.2.refs_2_), custom_call_target="tpu_custom_call" | custom-call | tf_op jit(solution)/shard_map/scatter/pallas_call | solution.py:543
  299.4 0.7 fusion
  300.1 0.1 slice.71
  300.3 1.1 pad_maximum_fusion.1
  (35 shorter events, 0.6 us)
Async XLA Ops:
  0.6 0.7 copy-start
  1.4 10.2 %collective-permute-start.1 = (s32[4]{0:T(128)S(1)}, s32[4]{0:T(128)S(1)}, u32[]{:S(2)}, u32[]{:S(2)}) collective-permute-start(s32[4]{0:T(128)S(1)} %slice_bitcast_fusion), channel_id=1, source_target_pairs={{4,0},{8,4},{12,8},{16,12},{20,16},{24,20},{28,24},{5,1},{9,5},{13... | collective-permute-start | bytes 56 | tf_op jit(solution)/shard_map/ppermute | solution.py:20
  2.7 8.9 %collective-permute-start.2 = (s32[4]{0:T(128)S(1)}, s32[4]{0:T(128)S(1)}, u32[]{:S(2)}, u32[]{:S(2)}) collective-permute-start(s32[4]{0:T(128)S(1)} %slice_bitcast_fusion), channel_id=1, source_target_pairs={{8,0},{12,4},{16,8},{20,12},{24,16},{28,20},{9,1},{13,5},{17,9},{2... | collective-permute-start | bytes 56 | tf_op jit(solution)/shard_map/ppermute | solution.py:20
  5.0 90.7 %collective-permute-start = (bf16[1,2,64,1024]{3,2,1,0:T(8,128)(2,1)S(1)}, bf16[1,2,64,1024]{3,2,1,0:T(8,128)(2,1)S(1)}, u32[]{:S(2)}, u32[]{:S(2)}) collective-permute-start(bf16[1,2,64,1024]{3,2,1,0:T(8,128)(2,1)S(1)} %fusion.3), channel_id=1, source_target_pairs={{0,1},{1,2},{2,3},{3,4},{4,5},{5,6},{6,7},{7,8},{8,9},{9,10},{10,1... | collective-permute-start | bytes 786440 | tf_op jit(solution)/shard_map/ppermute | solution.py:20
  11.7 106.3 %copy-start.4 = (s32[12]{0:T(128)}, s32[12]{0:T(128)S(1)}, u32[]{:S(2)}) copy-start(s32[12]{0:T(128)S(1)} %pad_add_fusion.1.wanted.index) | copy-start | bytes 148
  95.6 22.4 %copy-start.7 = (bf16[1,2,64,1024]{3,2,1,0:T(8,128)(2,1)}, bf16[1,2,64,1024]{3,2,1,0:T(8,128)(2,1)S(1)}, u32[]{:S(2)}) copy-start(bf16[1,2,64,1024]{3,2,1,0:T(8,128)(2,1)S(1)} %collective-permute-done.edge_ref) | copy-start | bytes 786436
  95.7 2.3 copy-start.5
  97.9 2.2 copy-start.6
  118.0 1.0 copy-start.8
  137.1 5.4 %copy-start.2 = (f32[2,64,512]{2,1,0:T(8,128)}, f32[2,64,512]{2,1,0:T(8,128)S(1)}, u32[]{:S(2)}) copy-start(f32[2,64,512]{2,1,0:T(8,128)S(1)} %get-tuple-element.31) | copy-start | bytes 786436
  137.1 23.7 %collective-permute-start.6 = (bf16[4,2,64,512]{3,2,1,0:T(8,128)(2,1)}, bf16[4,2,64,512]{3,2,1,0:T(8,128)(2,1)}, u32[]{:S(2)}, u32[]{:S(2)}) collective-permute-start(bf16[4,2,64,512]{3,2,1,0:T(8,128)(2,1)} %get-tuple-element.29.own_ref), channel_id=1, source_target_pairs={{8,0},{12,4},{16,8},{20,12},{24,16},{28,20},{9,1},{13,5},{17,9},{2... | collective-permute-start | bytes 1572872 | tf_op jit(solution)/shard_map/ppermute | solution.py:20
  138.4 22.4 %collective-permute-start.5 = (bf16[4,2,64,512]{3,2,1,0:T(8,128)(2,1)}, bf16[4,2,64,512]{3,2,1,0:T(8,128)(2,1)}, u32[]{:S(2)}, u32[]{:S(2)}) collective-permute-start(bf16[4,2,64,512]{3,2,1,0:T(8,128)(2,1)} %get-tuple-element.29.own_ref), channel_id=1, source_target_pairs={{4,0},{8,4},{12,8},{16,12},{20,16},{24,20},{28,24},{5,1},{9,5},{13... | collective-permute-start | bytes 1572872 | tf_op jit(solution)/shard_map/ppermute | solution.py:20
  139.7 39.4 %collective-permute-start.4 = (bf16[4,2,64,512]{3,2,1,0:T(8,128)(2,1)}, bf16[4,2,64,512]{3,2,1,0:T(8,128)(2,1)}, u32[]{:S(2)}, u32[]{:S(2)}) collective-permute-start(bf16[4,2,64,512]{3,2,1,0:T(8,128)(2,1)} %get-tuple-element.28.own_ref), channel_id=1, source_target_pairs={{8,0},{12,4},{16,8},{20,12},{24,16},{28,20},{9,1},{13,5},{17,9},{2... | collective-permute-start | bytes 1572872 | tf_op jit(solution)/shard_map/ppermute | solution.py:20
  141.0 38.1 %collective-permute-start.3 = (bf16[4,2,64,512]{3,2,1,0:T(8,128)(2,1)}, bf16[4,2,64,512]{3,2,1,0:T(8,128)(2,1)}, u32[]{:S(2)}, u32[]{:S(2)}) collective-permute-start(bf16[4,2,64,512]{3,2,1,0:T(8,128)(2,1)} %get-tuple-element.28.own_ref), channel_id=1, source_target_pairs={{4,0},{8,4},{12,8},{16,12},{20,16},{24,20},{28,24},{5,1},{9,5},{13... | collective-permute-start | bytes 1572872 | tf_op jit(solution)/shard_map/ppermute | solution.py:20
  142.5 1.3 copy-start.10
  143.8 4.2 %copy-start.3 = (f32[2,64,512]{2,1,0:T(8,128)S(1)}, f32[2,64,512]{2,1,0:T(8,128)}, u32[]{:S(2)}) copy-start(f32[2,64,512]{2,1,0:T(8,128)} %copy-done.2) | copy-start | bytes 786436
  143.8 8.5 %collective-permute-start.7 = (bf16[1,2,64,1024]{3,2,1,0:T(8,128)(2,1)S(1)}, bf16[1,2,64,1024]{3,2,1,0:T(8,128)(2,1)}, u32[]{:S(2)}, u32[]{:S(2)}) collective-permute-start(bf16[1,2,64,1024]{3,2,1,0:T(8,128)(2,1)S(1)} %slice.72), channel_id=1, source_target_pairs={{1,0},{2,1},{3,2},{4,3},{5,4},{6,5},{7,6},{8,7},{9,8},{10,9},{11,1... | collective-permute-start | bytes 786440 | tf_op jit(solution)/shard_map/ppermute | solution.py:20
  184.0 1.6 copy-start.1
  185.6 113.7 %copy-start.9 = (f32[3,2,64,1024]{3,2,1,0:T(8,128)S(1)}, f32[3,2,64,1024]{3,2,1,0:T(8,128)}, u32[]{:S(2)}) copy-start(f32[3,2,64,1024]{3,2,1,0:T(8,128)} %slice.40) | copy-start | bytes 4718596

commit v4 on v3

--- a/solution.py
+++ b/solution.py
@@ -253,8 +253,8 @@
     shard, part = lax.axis_index("seq"), lax.axis_index("head")
     blocks, _, _, width = own.shape
     count = wholes[0].shape[0]
-    head_steps, seq_steps = tree_steps(head_size), tree_steps(seq_size)
-    greet(head_steps, seq_steps, head_size, seq_size)
+    seq_steps = tree_steps(seq_size)
+    greet(range(1, head_size // 2 + 1), seq_steps, head_size, seq_size)
     right = jnp.minimum(part + 1, head_size - 1)
     left = jnp.maximum(part - 1, 0)
     for c in range(PIECES):
@@ -292,24 +292,37 @@
         def _():
             going_left(k, c).wait_recv()
 
-    events = [("head", step) for step in head_steps] + [("seq", step) for step in seq_steps]
-
-    def root_copy(e):
-        axis, step = events[e]
-        at, length = (part, head_size) if axis == "head" else (shard, seq_size)
-        other = jnp.minimum(at + step, length - 1)
-        copy = send(root, root, root_send.at[e], root_recv.at[e], axis, other)
-        takes_part = shard == 0 if axis == "head" else shard >= 0
-        gives = jnp.logical_and(takes_part, jnp.logical_and(at < step, at + step < length))
-        gets = jnp.logical_and(takes_part, jnp.logical_and(at >= step, at < 2 * step))
+    def root_over_head(z):
+        return send(root, root, root_send.at[z - 1], root_recv.at[z - 1], "head", z)
+
+    def root_over_seq(e):
+        step = seq_steps[e]
+        other = jnp.minimum(shard + step, seq_size - 1)
+        at = head_size - 1 + e
+        copy = send(root, root, root_send.at[at], root_recv.at[at], "seq", other)
+        gives = jnp.logical_and(shard < step, shard + step < seq_size)
+        gets = jnp.logical_and(shard >= step, shard < 2 * step)
         return copy, gives, gets
 
+    at_first = jnp.logical_and(shard == 0, part == 0)
+
+    @pl.when(at_first)
+    def _():
+        for z in range(1, head_size):
+            root_over_head(z).start()
+
     def root_event(e):
-        if 0 < e <= len(events):
-            copy, _, gets = root_copy(e - 1)
+        if e == 0:
+
+            @pl.when(jnp.logical_and(shard == 0, part > 0))
+            def _():
+                root_over_head(jnp.maximum(part, 1)).wait_recv()
+
+        elif e <= len(seq_steps):
+            copy, _, gets = root_over_seq(e - 1)
             pl.when(gets)(copy.wait_recv)
-        if e < len(events):
-            copy, gives, _ = root_copy(e)
+        if e < len(seq_steps):
+            copy, gives, _ = root_over_seq(e)
             pl.when(gives)(copy.start)
 
     done = 0
@@ -346,9 +359,7 @@
         for n in range(blocks):
             stage_near[c, n] = wholes[c][block_at(blocks + n)]
         pl.when(shard + 1 < seq_size)(near_copy(c).start)
-        root_event(done)
-        done += 1
-    while done <= len(events):
+    while done <= len(seq_steps):
         root_event(done)
         done += 1
     root_out[0] = root[...]
@@ -379,14 +390,19 @@
             pl.when(sends_left(k))(going_left(k, c).wait_send)
         pl.when(shard + 2 < seq_size)(far_copy(c).wait_send)
         pl.when(shard + 1 < seq_size)(near_copy(c).wait_send)
-    for e in range(len(events)):
-        copy, gives, _ = root_copy(e)
+    for e in range(len(seq_steps)):
+        copy, gives, _ = root_over_seq(e)
         pl.when(gives)(copy.wait_send)
+
+    @pl.when(at_first)
+    def _():
+        for z in range(1, head_size):
+            root_over_head(z).wait_send()
 
 
 def gather(wanted, back, own, head_size, seq_size):
     blocks, _, _, width = own.shape
-    events = len(tree_steps(head_size)) + len(tree_steps(seq_size))
+    events = head_size - 1 + len(tree_steps(seq_size))
     half = width * 2 // PIECES
     vmem, smem = pltpu.MemorySpace.VMEM, pltpu.MemorySpace.SMEM
     moved = pltpu.VMEM((PIECES, blocks, BLOCK, half), jnp.bfloat16)
@@ -427,8 +443,8 @@
      right_send, right_recv, left_send, left_recv, root_send, root_recv) = refs
     shard, part = lax.axis_index("seq"), lax.axis_index("head")
     blocks, _, _, width = out.shape
-    head_steps, seq_steps = tree_steps(head_size), tree_steps(seq_size)
-    greet(head_steps, seq_steps, head_size, seq_size)
+    seq_steps = tree_steps(seq_size)
+    greet(range(1, head_size // 2 + 1), seq_steps, head_size, seq_size)
     right = jnp.minimum(part + 1, head_size - 1)
     left = jnp.maximum(part - 1, 0)
     root[...] = root_in[...]
@@ -446,34 +462,44 @@
             source, left_in.at[d, c], left_send.at[d, c], left_recv.at[d, c], "head", left
         )
 
-    events = [("seq", step) for step in seq_steps[::-1]] + [
-        ("head", step) for step in head_steps[::-1]
-    ]
-
-    def root_copy(e):
-        axis, step = events[e]
-        at, length = (part, head_size) if axis == "head" else (shard, seq_size)
-        other = jnp.maximum(at - step, 0)
-        copy = send(root, root_box.at[e], root_send.at[e], root_recv.at[e], axis, other)
-        takes_part = shard == 0 if axis == "head" else shard >= 0
-        gives = jnp.logical_and(takes_part, jnp.logical_and(at >= step, at < 2 * step))
-        gets = jnp.logical_and(takes_part, jnp.logical_and(at < step, at + step < length))
+    seq_steps = seq_steps[::-1]
+
+    def root_over_seq(e):
+        step = seq_steps[e]
+        other = jnp.maximum(shard - step, 0)
+        at = head_size - 1 + e
+        copy = send(root, root_box.at[at], root_send.at[at], root_recv.at[at], "seq", other)
+        gives = jnp.logical_and(shard >= step, shard < 2 * step)
+        gets = jnp.logical_and(shard < step, shard + step < seq_size)
         return copy, gives, gets
 
+    def root_over_head(z):
+        return send(
+            root, root_box.at[z - 1], root_send.at[z - 1], root_recv.at[z - 1], "head", 0
+        )
+
+    gives_last = jnp.logical_and(shard == 0, part > 0)
+
     def root_event(e):
-        if 0 < e <= len(events):
-            copy, _, gets = root_copy(e - 1)
+        if 0 < e <= len(seq_steps):
+            copy, _, gets = root_over_seq(e - 1)
 
             @pl.when(gets)
             def _():
                 copy.wait_recv()
-                root[...] += root_box[e - 1]
-
-        if e < len(events):
-            copy, gives, _ = root_copy(e)
+                root[...] += root_box[head_size - 1 + e - 1]
+
+        if e < len(seq_steps):
+            copy, gives, _ = root_over_seq(e)
             pl.when(gives)(copy.start)
-
-    done = 0
+        elif e == len(seq_steps):
+
+            @pl.when(gives_last)
+            def _():
+                root_over_head(jnp.maximum(part, 1)).start()
+
+    root_event(0)
+    done = 1
     for k in range(1, head_size):
         to_right, to_left = head_size - k, k - 1
         for c in range(PIECES):
@@ -502,9 +528,10 @@
                 ).astype(jnp.bfloat16)
                 going_left(d, c, left_out.at[d, c]).start()
 
-            root_event(done)
-            done += 1
-    while done <= len(events):
+            if c % 2 == 1:
+                root_event(done)
+                done += 1
+    while done <= len(seq_steps):
         root_event(done)
         done += 1
     for c in range(PIECES):
@@ -521,21 +548,31 @@
             going_left(part, c, left_out.at[part, c]).wait_recv()
             out[:, kv, :, columns] += left_in[part, c].astype(jnp.float32)
 
+    @pl.when(jnp.logical_and(shard == 0, part == 0))
+    def _():
+        for z in range(1, head_size):
+            root_over_head(z).wait_recv()
+            root[...] += root_box[z - 1]
+
     root_out[...] = root[...]
     for d in range(head_size):
         for c in range(PIECES):
             pl.when(part < d)(going_right(d, c, right_out.at[d, c]).wait_send)
             pl.when(part > d)(going_left(d, c, left_out.at[d, c]).wait_send)
-    for e in range(len(events)):
-        copy, gives, _ = root_copy(e)
+    for e in range(len(seq_steps)):
+        copy, gives, _ = root_over_seq(e)
         pl.when(gives)(copy.wait_send)
+
+    @pl.when(gives_last)
+    def _():
+        root_over_head(jnp.maximum(part, 1)).wait_send()
 
 
 def scatter(placed, root, head_size, seq_size):
     count = placed[0].shape[0]
     width = root.shape[-1]
     blocks = count // head_size
-    events = len(tree_steps(head_size)) + len(tree_steps(seq_size))
+    events = head_size - 1 + len(tree_steps(seq_size))
     half = width * 2 // PIECES
     vmem = pltpu.MemorySpace.VMEM
     box = pltpu.VMEM((head_size, PIECES, blocks, BLOCK, half), jnp.bfloat16)

time: 302 us -> 295 us (0.977); the launches traced: 301 us -> 291 us
  Pallas kernels: 244 us -> 234 us
    pallas_call x1, Pallas kernels: 114 us -> 104 us  [scatter(): pl.pallas_call(functools.partial(scatter_kernel, head_size, seq_size), in...]
  transfers between devices with their start and end apart: 8 -> 8, of which waited for: 3 -> 3; matrix products, arithmetic and copies ran while one was open for 2% -> 2% of each run, Pallas kernels for 29% -> 31%
where the time goes in v4:
time: 295 us; the launch traced here: 291 us
  Pallas kernels  234 us (79%)
  waiting for transfers between devices  24.2 us (8%)
  starting transfers between devices  14.1 us (5%)
  local copies, waits for them, and re-layouts  12.3 us (4%)
  other arithmetic  5.37 us (2%)
    pallas_call x1, Pallas kernels, scatter(): pl.pallas_call(functools.partial(scatter_kernel, head_size, seq_size), in...  104 us
    pallas_call x1, Pallas kernels, gather(): pl.pallas_call(functools.partial(gather_kernel, head_size, seq_size), in_...  84.4 us
    pallas_call x2, Pallas kernels, attention(): pl.pallas_call(functools.partial(attention_kernel, groups=groups, aliased...  36 us
    ppermute x8, waiting for transfers between devices, shifted(): return lax.ppermute(x, axis, pairs)  24.2 us
    ppermute x8, starting transfers between devices, shifted(): return lax.ppermute(x, axis, pairs)  14.1 us
    pallas_call x2, Pallas kernels, place(): pl.pallas_call(place_kernel, grid_spec=pltpu.PrefetchScalarGridSpec(num_s...  9.91 us
    unnamed x23, local copies, waits for them, and re-layouts  9.06 us
  transfers between devices with their start and end apart: 8, of which 3 were waited for; matrix products, arithmetic and copies ran while one was open for 2% of the time, Pallas kernels for 31%

profile of v4, /device:TPU:0, one launch (start us, length us, event | category | flops | bytes accessed | tf_op | source)
XLA Modules:
  0.0 291.0 jit_solution(17621692527545733733)
XLA Ops:
  0.7 0.7 copy-done
  1.4 1.3 collective-permute-start.1
  2.7 1.3 collective-permute-start.2
  4.0 1.0 fusion.3
  5.0 4.9 %collective-permute-start = (bf16[1,2,64,1024]{3,2,1,0:T(8,128)(2,1)S(1)}, bf16[1,2,64,1024]{3,2,1,0:T(8,128)(2,1)S(1)}, u32[]{:S(2)}, u32[]{:S(2)}) collective-permute-start(bf16[1,2,64,1024]{3,2,1,0:T(8,128)(2,1)S(1)} %fusion.3), channel_id=1, source_target_pairs={{0,1},{1,2},{2,3},{3,4},{4,5},{5,6},{6,7},{7,8},{8,9},{9,10},{10,1... | collective-permute-start | bytes 786440 | tf_op jit(solution)/shard_map/ppermute | solution.py:20
  10.0 1.3 pad_maximum_fusion.own.own_ref.before_ref
  11.3 0.1 copy.12
  11.7 84.4 %gather.1 = (bf16[4,2,64,1024]{3,2,1,0:T(8,128)(2,1)S(1)}, bf16[1,2,64,1024]{3,2,1,0:T(8,128)(2,1)S(1)}) custom-call(s32[12]{0:T(128)S(1)} %pad_add_fusion.1.wanted.index, s32[4]{0:T(128)S(1)} %get-tuple-element.38.back, bf16[4,2,64,1024]{3,2,1,0:T(8,128)(2,1)S(1)} %pad_maximum_fusion.own.own_ref.before_ref), custom_call_target="tpu_custom_call" | custom-call | tf_op jit(solution)/shard_map/gather/pallas_call | solution.py:411
  96.1 2.3 copy-done.5
  98.4 2.2 copy-done.6
  100.6 17.9 %attention.2 = (bf16[256,8192]{1,0:T(8,128)(2,1)}, bf16[256,8192]{1,0:T(8,128)(2,1)}, f32[4,2,64,512]{3,2,1,0:T(8,128)S(1)}, f32[4,2,64,512]{3,2,1,0:T(8,128)S(1...) custom-call(s32[9]{0:T(128)S(1)} %pad_add_fusion.info, bf16[256,8192]{1,0:T(8,128)(2,1)S(1)} %copy-done.5, ...), custom_call_target="tpu_custom_call" | custom-call | flops 21474836480 | bytes 8388608 | tf_op jit(solution)/shard_map/attention/pallas_call | solution.py:129
  118.5 0.9 copy-done.8
  119.4 18.1 %attention.3 = (bf16[256,8192]{1,0:T(8,128)(2,1)}, bf16[256,8192]{1,0:T(8,128)(2,1)}, f32[4,2,64,512]{3,2,1,0:T(8,128)S(1)}, f32[4,2,64,512]{3,2,1,0:T(8,128)S(1...) custom-call(s32[9]{0:T(128)S(1)} %pad_add_fusion.info, ...), custom_call_target="tpu_custom_call", output_to_operand_aliasing={{0}: (8, {}), {1}: (9, {})} | custom-call | flops 21474836480 | bytes 8388608 | tf_op jit(solution)/shard_map/attention/pallas_call | solution.py:129
  137.6 1.3 collective-permute-start.6
  138.8 1.3 collective-permute-start.5
  140.1 1.3 collective-permute-start.4
  141.4 1.3 collective-permute-start.3
  142.8 0.1 constant_dynamic-update-slice_fusion
  143.0 1.3 copy-done.10
  144.3 1.4 collective-permute-start.7
  145.7 2.8 slice.40
  148.5 4.3 %collective-permute-done.7 = bf16[1,2,64,1024]{3,2,1,0:T(8,128)(2,1)} collective-permute-done((bf16[1,2,64,1024]{3,2,1,0:T(8,128)(2,1)S(1)}, bf16[1,2,64,1024]{3,2,1,0:T(8,128)(2,1)}, u32[]{:S(2)}, u32[]{:S(2)}) %collective-permute-start.7) | collective-permute-done | bytes 262176 | tf_op jit(solution)/shard_map/ppermute | solution.py:20
  152.8 1.0 convert_element_type.13
  153.8 6.2 %collective-permute-done.6.far_ref = bf16[4,2,64,512]{3,2,1,0:T(8,128)(2,1)} collective-permute-done((bf16[4,2,64,512]{3,2,1,0:T(8,128)(2,1)}, bf16[4,2,64,512]{3,2,1,0:T(8,128)(2,1)}, u32[]{:S(2)}, u32[]{:S(2)}) %collective-permute-start.6) | collective-permute-done | bytes 524320 | tf_op jit(solution)/shard_map/ppermute | solution.py:20
  160.0 5.0 %place.3.refs_1_ = bf16[16,2,64,512]{3,2,1,0:T(8,128)(2,1)} custom-call(s32[12]{0:T(128)} %copy-done.4, bf16[4,2,64,512]{3,2,1,0:T(8,128)(2,1)} %get-tuple-element.29.own_ref, bf16[4,2,64,512]{3,2,1,0:T(8,128)(2,1)} %collective-permute-done.5.near_ref, bf16[4,2,64,512]{3,2,1,0:T(8,128)(2,1)} %collective-permute-done.6.far_ref), custom_call_target="tpu_custom_call" | custom-call | flops 1048576 | bytes 3670016 | tf_op jit(solution)/shard_map/place/pallas_call | solution.py:183
  164.9 13.8 %collective-permute-done.4.far_ref = bf16[4,2,64,512]{3,2,1,0:T(8,128)(2,1)} collective-permute-done((bf16[4,2,64,512]{3,2,1,0:T(8,128)(2,1)}, bf16[4,2,64,512]{3,2,1,0:T(8,128)(2,1)}, u32[]{:S(2)}, u32[]{:S(2)}) %collective-permute-start.4) | collective-permute-done | bytes 524320 | tf_op jit(solution)/shard_map/ppermute | solution.py:20
  178.7 5.0 %place.2.refs_0_ = bf16[16,2,64,512]{3,2,1,0:T(8,128)(2,1)} custom-call(s32[12]{0:T(128)} %copy-done.4, bf16[4,2,64,512]{3,2,1,0:T(8,128)(2,1)} %get-tuple-element.28.own_ref, bf16[4,2,64,512]{3,2,1,0:T(8,128)(2,1)} %collective-permute-done.3.near_ref, bf16[4,2,64,512]{3,2,1,0:T(8,128)(2,1)} %collective-permute-done.4.far_ref), custom_call_target="tpu_custom_call" | custom-call | flops 1048576 | bytes 3670016 | tf_op jit(solution)/shard_map/place/pallas_call | solution.py:183
  183.6 1.6 copy-done.1
  185.2 103.7 %scatter.1 = (f32[4,2,64,1024]{3,2,1,0:T(8,128)S(1)}, f32[2,64,1024]{2,1,0:T(8,128)S(1)}) custom-call(bf16[16,2,64,512]{3,2,1,0:T(8,128)(2,1)S(1)} %copy-done.1, bf16[16,2,64,512]{3,2,1,0:T(8,128)(2,1)} %place.3.refs_1_, f32[2,64,1024]{2,1,0:T(8,128)S(1)} %pad_maximum_fusion.2.refs_2_), custom_call_target="tpu_custom_call" | custom-call | tf_op jit(solution)/shard_map/scatter/pallas_call | solution.py:580
  289.0 0.7 fusion
  289.7 0.1 slice.71
  289.9 1.1 pad_maximum_fusion.1
  (35 shorter events, 0.6 us)
Async XLA Ops:
  0.6 0.7 copy-start
  1.4 10.2 %collective-permute-start.1 = (s32[4]{0:T(128)S(1)}, s32[4]{0:T(128)S(1)}, u32[]{:S(2)}, u32[]{:S(2)}) collective-permute-start(s32[4]{0:T(128)S(1)} %slice_bitcast_fusion), channel_id=1, source_target_pairs={{4,0},{8,4},{12,8},{16,12},{20,16},{24,20},{28,24},{5,1},{9,5},{13... | collective-permute-start | bytes 56 | tf_op jit(solution)/shard_map/ppermute | solution.py:20
  2.7 8.9 %collective-permute-start.2 = (s32[4]{0:T(128)S(1)}, s32[4]{0:T(128)S(1)}, u32[]{:S(2)}, u32[]{:S(2)}) collective-permute-start(s32[4]{0:T(128)S(1)} %slice_bitcast_fusion), channel_id=1, source_target_pairs={{8,0},{12,4},{16,8},{20,12},{24,16},{28,20},{9,1},{13,5},{17,9},{2... | collective-permute-start | bytes 56 | tf_op jit(solution)/shard_map/ppermute | solution.py:20
  5.0 91.1 %collective-permute-start = (bf16[1,2,64,1024]{3,2,1,0:T(8,128)(2,1)S(1)}, bf16[1,2,64,1024]{3,2,1,0:T(8,128)(2,1)S(1)}, u32[]{:S(2)}, u32[]{:S(2)}) collective-permute-start(bf16[1,2,64,1024]{3,2,1,0:T(8,128)(2,1)S(1)} %fusion.3), channel_id=1, source_target_pairs={{0,1},{1,2},{2,3},{3,4},{4,5},{5,6},{6,7},{7,8},{8,9},{9,10},{10,1... | collective-permute-start | bytes 786440 | tf_op jit(solution)/shard_map/ppermute | solution.py:20
  11.7 106.8 %copy-start.4 = (s32[12]{0:T(128)}, s32[12]{0:T(128)S(1)}, u32[]{:S(2)}) copy-start(s32[12]{0:T(128)S(1)} %pad_add_fusion.1.wanted.index) | copy-start | bytes 148
  96.1 22.4 %copy-start.7 = (bf16[1,2,64,1024]{3,2,1,0:T(8,128)(2,1)}, bf16[1,2,64,1024]{3,2,1,0:T(8,128)(2,1)S(1)}, u32[]{:S(2)}) copy-start(bf16[1,2,64,1024]{3,2,1,0:T(8,128)(2,1)S(1)} %collective-permute-done.edge_ref) | copy-start | bytes 786436
  96.1 2.3 copy-start.5
  98.4 2.2 copy-start.6
  118.5 1.0 copy-start.8
  137.6 5.4 %copy-start.2 = (f32[2,64,512]{2,1,0:T(8,128)}, f32[2,64,512]{2,1,0:T(8,128)S(1)}, u32[]{:S(2)}) copy-start(f32[2,64,512]{2,1,0:T(8,128)S(1)} %get-tuple-element.31) | copy-start | bytes 786436
  137.6 22.4 %collective-permute-start.6 = (bf16[4,2,64,512]{3,2,1,0:T(8,128)(2,1)}, bf16[4,2,64,512]{3,2,1,0:T(8,128)(2,1)}, u32[]{:S(2)}, u32[]{:S(2)}) collective-permute-start(bf16[4,2,64,512]{3,2,1,0:T(8,128)(2,1)} %get-tuple-element.29.own_ref), channel_id=1, source_target_pairs={{8,0},{12,4},{16,8},{20,12},{24,16},{28,20},{9,1},{13,5},{17,9},{2... | collective-permute-start | bytes 1572872 | tf_op jit(solution)/shard_map/ppermute | solution.py:20
  138.8 21.1 %collective-permute-start.5 = (bf16[4,2,64,512]{3,2,1,0:T(8,128)(2,1)}, bf16[4,2,64,512]{3,2,1,0:T(8,128)(2,1)}, u32[]{:S(2)}, u32[]{:S(2)}) collective-permute-start(bf16[4,2,64,512]{3,2,1,0:T(8,128)(2,1)} %get-tuple-element.29.own_ref), channel_id=1, source_target_pairs={{4,0},{8,4},{12,8},{16,12},{20,16},{24,20},{28,24},{5,1},{9,5},{13... | collective-permute-start | bytes 1572872 | tf_op jit(solution)/shard_map/ppermute | solution.py:20
  140.1 38.5 %collective-permute-start.4 = (bf16[4,2,64,512]{3,2,1,0:T(8,128)(2,1)}, bf16[4,2,64,512]{3,2,1,0:T(8,128)(2,1)}, u32[]{:S(2)}, u32[]{:S(2)}) collective-permute-start(bf16[4,2,64,512]{3,2,1,0:T(8,128)(2,1)} %get-tuple-element.28.own_ref), channel_id=1, source_target_pairs={{8,0},{12,4},{16,8},{20,12},{24,16},{28,20},{9,1},{13,5},{17,9},{2... | collective-permute-start | bytes 1572872 | tf_op jit(solution)/shard_map/ppermute | solution.py:20
  141.4 37.2 %collective-permute-start.3 = (bf16[4,2,64,512]{3,2,1,0:T(8,128)(2,1)}, bf16[4,2,64,512]{3,2,1,0:T(8,128)(2,1)}, u32[]{:S(2)}, u32[]{:S(2)}) collective-permute-start(bf16[4,2,64,512]{3,2,1,0:T(8,128)(2,1)} %get-tuple-element.28.own_ref), channel_id=1, source_target_pairs={{4,0},{8,4},{12,8},{16,12},{20,16},{24,20},{28,24},{5,1},{9,5},{13... | collective-permute-start | bytes 1572872 | tf_op jit(solution)/shard_map/ppermute | solution.py:20
  142.9 1.3 copy-start.10
  144.3 4.2 %copy-start.3 = (f32[2,64,512]{2,1,0:T(8,128)S(1)}, f32[2,64,512]{2,1,0:T(8,128)}, u32[]{:S(2)}) copy-start(f32[2,64,512]{2,1,0:T(8,128)} %copy-done.2) | copy-start | bytes 786436
  144.3 8.5 %collective-permute-start.7 = (bf16[1,2,64,1024]{3,2,1,0:T(8,128)(2,1)S(1)}, bf16[1,2,64,1024]{3,2,1,0:T(8,128)(2,1)}, u32[]{:S(2)}, u32[]{:S(2)}) collective-permute-start(bf16[1,2,64,1024]{3,2,1,0:T(8,128)(2,1)S(1)} %slice.72), channel_id=1, source_target_pairs={{1,0},{2,1},{3,2},{4,3},{5,4},{6,5},{7,6},{8,7},{9,8},{10,9},{11,1... | collective-permute-start | bytes 786440 | tf_op jit(solution)/shard_map/ppermute | solution.py:20
  183.6 1.6 copy-start.1
  185.2 103.8 %copy-start.9 = (f32[3,2,64,1024]{3,2,1,0:T(8,128)S(1)}, f32[3,2,64,1024]{3,2,1,0:T(8,128)}, u32[]{:S(2)}) copy-start(f32[3,2,64,1024]{3,2,1,0:T(8,128)} %slice.40) | copy-start | bytes 4718596
